TPU v7x, 32 devices: a whole 2x2x4 slice. The times are simulated.
32 devices in a mesh: lat: 4 (over x, core), lon: 8 (over z, y).
Axes of the slice: x: 2, y: 2, z: 4, core: 2. Of those that a mesh axis runs over, the one named last changes fastest.
Arguments:
- start_state: float32 [256, 64, 1024], P('lat', None, 'lon'), may hold values from -6 to 6
- coefficients: float32 [5, 64], replicated, may hold values from 0.05 to 0.35
- w_in: bfloat16 [64, 512], replicated, may hold values from -0.75 to 0.75
- w_out: bfloat16 [512, 64], replicated, may hold values from -0.25 to 0.25
- jacobian: float32 [128, 64], replicated, may hold values from -0.75 to 0.75
- sigma: float32 [128], replicated, may hold values from 0.5 to 2
- obs_values: float32 [8192, 128], P(('lat', 'lon')), may hold values from -6 to 6
- owner: int32 [8192, 1], P(('lat', 'lon')), may hold values from 0 to 31; in each aligned block of 256 rows (0 to 255, 256 to 511, ...) at most 16 rows name the same one
- stencil: int32 [8192, 4], P(('lat', 'lon')), may hold values from 0 to 8191
- counts: int32 [8192], P(('lat', 'lon')), may hold values from 1 to 128
Outputs:
- grad_state: float32 [256, 64, 1024], P('lat', None, 'lon')
- departures: float32 [8192, 128], P(('lat', 'lon'))
- grad_w_in: float32 [64, 512], replicated
- grad_w_out: float32 [512, 64], replicated
Inputs may be any that keep to these rules, and one draw needn't show every extreme that they name: owner is the tile's index lat * 8 + lon. Among the rows of one device no tile is named by more than 16 rows, a bound that some block reaches. `stencil`: A cell index inside the owning tile is its row times 128 plus its column.
All inputs are finite; a program needn't handle non-finite values.
Results may differ from a plain program's by a relative error of at most 0.0018.
The roundings to bfloat16 on the way count: a program that leaves them out, or rounds other values in their place, can miss the bound.
Values sent between devices are 32-bit elements; how exact they have to be, the bound alone decides.
A program may use at most 128 MiB of HBM per device.

v0:
```python
import math

import jax
import jax.numpy as jnp
from jax import lax
from jax.sharding import PartitionSpec as P

CAP = 16


interp_weights = (0.4, 0.3, 0.2, 0.1)


def padded(shard, sides, width, wrap):
    for axis, dim in sides:
        peers, length = (lax.axis_size(axis), shard.shape[dim])
        up = [(i, (i + 1) % peers) for i in range(peers if wrap else peers - 1)]
        down = [(j, i) for i, j in up]
        last = lax.slice_in_dim(shard, length - width, length, axis=dim)
        initial = lax.slice_in_dim(shard, 0, width, axis=dim)
        before = lax.ppermute(last, axis, up)
        after = lax.ppermute(initial, axis, down)
        shard = jnp.concatenate([before, shard, after], axis=dim)
    return shard


def group_size(nrows, width, target):
    group = max(1, min(nrows, target // width))
    while nrows % group:
        group -= 1
    return group


def stencil_apply(extended, coefficients):
    scaled = coefficients[:, None, :, None]
    centre = extended[1:-1, :, 1:-1]
    return (
        scaled[0] * centre
        + scaled[1] * extended[:-2, :, 1:-1]
        + scaled[2] * extended[2:, :, 1:-1]
        + scaled[3] * extended[1:-1, :, :-2]
        + scaled[4] * extended[1:-1, :, 2:]
    )


def stencil_adjoint(extended, coefficients):
    scaled = coefficients[:, None, :, None]
    centre = extended[1:-1, :, 1:-1]
    return (
        scaled[0] * centre
        + scaled[1] * extended[2:, :, 1:-1]
        + scaled[2] * extended[:-2, :, 1:-1]
        + scaled[3] * extended[1:-1, :, 2:]
        + scaled[4] * extended[1:-1, :, :-2]
    )


def closure_block(block, w_in, w_out):
    inputs = block.astype(jnp.bfloat16)
    pre = jnp.einsum("fh,gfw->ghw", w_in, inputs, preferred_element_type=jnp.float32)
    hidden = jnp.tanh(pre).astype(jnp.bfloat16)
    return jnp.einsum("hf,ghw->gfw", w_out, hidden, preferred_element_type=jnp.float32)


def closure_forward(state, w_in, w_out):
    nrows, feat, width = state.shape
    group = group_size(nrows, width, 2048)
    blocks = state.reshape(nrows // group, group, feat, width)
    result = lax.map(lambda block: closure_block(block, w_in, w_out), blocks)
    return result.reshape(nrows, feat, width)


def closure_backward(state, cotangent, w_in, w_out):
    nrows, feat, width = state.shape
    group = group_size(nrows, width, 2048)
    blocks = state.reshape(nrows // group, group, feat, width)
    cot_blocks = cotangent.reshape(nrows // group, group, feat, width)

    def one_block(carry, pieces):
        block, cot_block = pieces
        inputs = block.astype(jnp.bfloat16)
        pre = jnp.einsum("fh,gfw->ghw", w_in, inputs, preferred_element_type=jnp.float32)
        tanh_pre = jnp.tanh(pre)
        hidden = tanh_pre.astype(jnp.bfloat16)
        cot_low = cot_block.astype(jnp.bfloat16)
        grad_out = jnp.einsum("ghw,gfw->hf", hidden, cot_low, preferred_element_type=jnp.float32)
        back_hidden = jnp.einsum("hf,gfw->ghw", w_out, cot_low, preferred_element_type=jnp.float32)
        back_pre = (back_hidden * (1.0 - tanh_pre * tanh_pre)).astype(jnp.bfloat16)
        grad_in = jnp.einsum("gfw,ghw->fh", inputs, back_pre, preferred_element_type=jnp.float32)
        back_state = jnp.einsum("fh,ghw->gfw", w_in, back_pre, preferred_element_type=jnp.float32)
        return ((carry[0] + grad_in, carry[1] + grad_out), back_state)

    init = (
        jnp.zeros((feat, w_in.shape[1]), jnp.float32),
        jnp.zeros((w_in.shape[1], feat), jnp.float32),
    )
    totals, back = lax.scan(one_block, init, (blocks, cot_blocks))
    return (back.reshape(nrows, feat, width), totals[0], totals[1])


def extend_forward(state):
    wider = padded(state, (("lon", 2),), 1, True)
    return padded(wider, (("lat", 0),), 1, False)


def extend_adjoint(field):
    wider = padded(field, (("lon", 2),), 1, True)
    return padded(wider, (("lat", 0),), 1, False)


def interpolate(state_two, cell_rows, cell_cols):
    interp = interp_weights[0] * state_two[cell_rows[:, 0], :, cell_cols[:, 0]]
    for corner in range(1, 4):
        interp = (
            interp
            + interp_weights[corner] * state_two[cell_rows[:, corner], :, cell_cols[:, corner]]
        )
    return interp


def spread_back(like, cell_rows, cell_cols, pulled):
    adjoint_two = jnp.zeros_like(like)
    for corner in range(4):
        adjoint_two = adjoint_two.at[cell_rows[:, corner], :, cell_cols[:, corner]].add(
            interp_weights[corner] * pulled
        )
    return adjoint_two


def on_device(
    start_state, coefficients, w_in, w_out, jacobian, sigma, obs_values, owner, stencil, counts
):
    tlat, feat, tlon = start_state.shape
    lat_count = lax.axis_size("lat")
    lon_count = lax.axis_size("lon")
    devices = lat_count * lon_count
    channels = obs_values.shape[1]
    tile_owner = owner[:, 0]
    onehot = (tile_owner[:, None] == jnp.arange(devices, dtype=jnp.int32)[None, :]).astype(
        jnp.int32
    )
    running = jnp.cumsum(onehot, axis=0)
    rank = jnp.sum(running * onehot, axis=1) - 1
    slot = tile_owner * CAP + rank
    slots = devices * CAP
    send_stencil = jnp.zeros((slots, 4), jnp.int32).at[slot].set(stencil)
    channel_ids = jnp.arange(channels, dtype=jnp.int32)
    cell_recv = lax.all_to_all(
        send_stencil, ("lat", "lon"), split_axis=0, concat_axis=0, tiled=True
    )
    state_one = stencil_apply(extend_forward(start_state), coefficients) + closure_forward(
        start_state, w_in, w_out
    )
    state_two = stencil_apply(extend_forward(state_one), coefficients) + closure_forward(
        state_one, w_in, w_out
    )
    cell_rows = cell_recv // tlon
    cell_cols = cell_recv % tlon
    slot_interp = interpolate(state_two, cell_rows, cell_cols)
    returned_interp = lax.all_to_all(
        slot_interp, ("lat", "lon"), split_axis=0, concat_axis=0, tiled=True
    )
    row_interp = returned_interp[slot]
    evolved = jnp.dot(
        row_interp, jacobian.T, precision=lax.Precision.HIGHEST, preferred_element_type=jnp.float32
    )
    used = channel_ids[None, :] < counts[:, None]
    departures = jnp.where(used, (obs_values - evolved) / sigma[None, :], 0.0)
    row_pulled = jnp.dot(
        -departures / sigma[None, :],
        jacobian,
        precision=lax.Precision.HIGHEST,
        preferred_element_type=jnp.float32,
    )
    send_pulled = jnp.zeros((slots, feat), jnp.float32).at[slot].set(row_pulled)
    recv_pulled = lax.all_to_all(
        send_pulled, ("lat", "lon"), split_axis=0, concat_axis=0, tiled=True
    )
    adjoint_two = spread_back(state_two, cell_rows, cell_cols, recv_pulled)
    back_one, gin_one, gout_one = closure_backward(state_one, adjoint_two, w_in, w_out)
    adjoint_one = stencil_adjoint(extend_adjoint(adjoint_two), coefficients) + back_one
    back_zero, gin_zero, gout_zero = closure_backward(start_state, adjoint_one, w_in, w_out)
    grad_state = stencil_adjoint(extend_adjoint(adjoint_one), coefficients) + back_zero
    grad_in, grad_out = lax.psum((gin_one + gin_zero, gout_one + gout_zero), ("lat", "lon"))
    scale = 1.0 / math.sqrt(tlat * lat_count * tlon * lon_count)
    return (grad_state, departures, grad_in * scale, grad_out * scale)


def solution(mesh):
    return jax.shard_map(
        on_device,
        mesh=mesh,
        in_specs=(
            P("lat", None, "lon"),
            P(),
            P(),
            P(),
            P(),
            P(),
            P(("lat", "lon"), None),
            P(("lat", "lon"), None),
            P(("lat", "lon"), None),
            P(("lat", "lon")),
        ),
        out_specs=(P("lat", None, "lon"), P(("lat", "lon"), None), P(), P()),
        check_vma=False,
    )
```

profile of v0, /device:TPU:0, one launch (start us, length us, event | category | flops | bytes accessed | tf_op | source)
XLA Modules:
  0.0 733.6 jit_solution(17670146646272283155)
XLA Ops:
  7.2 3.9 copy.71
  12.3 3.0 collective-permute-start
  15.3 3.1 collective-permute-start.1
  21.6 3.3 all-to-all-start
  25.4 5.4 while.50
  30.8 2.7 copy.77
  38.7 2.7 collective-permute-done.3
  41.5 6.1 fusion.139
  51.1 3.3 collective-permute-start.5
  55.6 2.6 copy.78
  59.1 4.3 collective-permute-start.6
  66.5 8.5 %while.51 = (s32[]{:T(128)}, f32[4,16,64,128]{3,2,1,0:T(8,128)}, bf16[4,16,64,128]{3,2,1,0:T(8,128)(2,1)S(1)}, bf16[64,512]{1,0:T(8,128)(2,1)S(1)}, bf16[512,64]{0,1:T(8,128)(2,1)S(1)}, /*index=5*/s32[]{:T(128)}) while((s32[]{:T(128)}, f32[4,16,64,128]{3,2,1,0:T(8,128)}, bf16[4,16,64,128]{3,2,1,0:T(8,128)(2,1)S(1)}, ...), condition=%wide.region_7.8_spmd, body=%wide.region_6.7_spmd.sunk | while | flops 269484032 | bytes 918597 | solution.py:69
  75.0 3.8 copy.79
  78.8 14.8 %fusion.130 = f32[64,64,128]{1,2,0:T(8,128)} fusion(f32[64,64,1]{1,2,0:T(1,128)S(1)} %collective-permute-done.5, f32[64,64,128]{1,2,0:T(8,128)} %copy-done.5, f32[64,64,1]{1,2,0:T(1,128)S(1)} %collective-permute-done.4, f32[1,64,130]{1,2,0:T(8,128)S(1)} %collective-permute-done.7, f32[1,64,130]{1,2,0:T(8,128)S(1)} %collective-permute-done.6, ...), kind=kLoop, calls=%fused_computation.120 | loop fusion | flops 9437184 | bytes 6392064 | tf_op jit(solution)/shard_map/add | solution.py:154
  93.6 12.3 %gather_fusion = f32[512,64]{1,0:T(8,128)S(1)} fusion(f32[64,64,128]{1,2,0:T(8,128)} %fusion.130, s32[512]{0:T(512)S(1)} %get-tuple-element.287), kind=kCustom, calls=%fused_computation | custom fusion | bytes 266240 | tf_op jit(solution)/shard_map/gather | solution.py:112
  105.9 12.4 %gather_fusion.1 = f32[512,64]{1,0:T(8,128)S(1)} fusion(f32[64,64,128]{1,2,0:T(8,128)} %fusion.130, s32[512]{0:T(512)S(1)} %get-tuple-element.286), kind=kCustom, calls=%fused_computation.1 | custom fusion | bytes 266240 | tf_op jit(solution)/shard_map/gather | solution.py:116
  118.3 12.4 %gather_fusion.2 = f32[512,64]{1,0:T(8,128)S(1)} fusion(f32[64,64,128]{1,2,0:T(8,128)} %fusion.130, s32[512]{0:T(512)S(1)} %get-tuple-element.285), kind=kCustom, calls=%fused_computation.2 | custom fusion | bytes 266240 | tf_op jit(solution)/shard_map/gather | solution.py:116
  130.7 14.7 %gather_fusion.3 = f32[512,64]{1,0:T(8,128)} fusion(f32[64,64,128]{1,2,0:T(8,128)} %fusion.130, s32[512]{0:T(512)S(1)} %get-tuple-element.284), kind=kCustom, calls=%fused_computation.3 | custom fusion | bytes 266240 | tf_op jit(solution)/shard_map/gather | solution.py:116
  148.9 22.5 %all-to-all-start.1 = ((f32[32,1,1024]{2,1,0:T(1,128)}), f32[32,1,1024]{2,1,0:T(1,128)S(1)}, u32[]{:S(2)}, u32[]{:S(2)}) async-start(f32[32,1,1024]{2,1,0:T(1,128)} %reshape.217), calls=%async_computation.1 | async-start | bytes 262144 | tf_op jit(solution)/shard_map/all_to_all | solution.py:160
  171.5 7.7 %all-to-all-done.1 = f32[32,1,1024]{2,1,0:T(1,128)S(1)} async-done(((f32[32,1,1024]{2,1,0:T(1,128)}), f32[32,1,1024]{2,1,0:T(1,128)S(1)}, u32[]{:S(2)}, u32[]{:S(2)}) %all-to-all-start.1) | async-done | bytes 131104 | tf_op jit(solution)/shard_map/all_to_all | solution.py:160
  184.1 10.0 %all_to_all.30 = f32[32,1,1024]{2,1,0:T(1,128)S(1)} all-to-all(f32[32,1,1024]{2,1,0:T(1,128)S(1)} %reshape.219), channel_id=1, replica_groups=mesh['lat'=4,'lon'=8] {'lat','lon'}, dimensions={0} | all-to-all | bytes 262144 | tf_op jit(solution)/shard_map/all_to_all | solution.py:176
  197.6 2.5 broadcast_in_dim.20
  200.1 58.5 %scatter_fusion = f32[64,64,128]{1,2,0:T(8,128)} fusion(f32[64,64,128]{1,2,0:T(8,128)} %broadcast_in_dim.20, s32[512]{0:T(512)S(1)} %get-tuple-element.290, f32[512,64]{1,0:T(8,128)} %bitcast.306), kind=kCustom, calls=%fused_computation.7 | custom fusion | flops 32768 | bytes 397312 | tf_op jit(solution)/shard_map/scatter-add | solution.py:124
  258.6 58.4 %scatter_fusion.1 = f32[64,64,128]{1,2,0:T(8,128)} fusion(f32[64,64,128]{1,2,0:T(8,128)} %scatter_fusion, s32[512]{0:T(512)S(1)} %get-tuple-element.289, f32[512,64]{1,0:T(8,128)S(1)} %bitcast.305), kind=kCustom, calls=%fused_computation.8 | custom fusion | flops 32768 | bytes 397312 | tf_op jit(solution)/shard_map/scatter-add | solution.py:124
  317.0 58.4 %scatter_fusion.2 = f32[64,64,128]{1,2,0:T(8,128)} fusion(f32[64,64,128]{1,2,0:T(8,128)} %scatter_fusion.1, s32[512]{0:T(512)S(1)} %get-tuple-element.288, f32[512,64]{1,0:T(8,128)S(1)} %bitcast.304), kind=kCustom, calls=%fused_computation.9 | custom fusion | flops 32768 | bytes 397312 | tf_op jit(solution)/shard_map/scatter-add | solution.py:124
  375.5 58.4 %scatter_fusion.3 = f32[64,64,128]{1,2,0:T(8,128)} fusion(f32[64,64,128]{1,2,0:T(8,128)} %scatter_fusion.2, s32[512]{0:T(512)S(1)} %get-tuple-element.283, f32[512,64]{1,0:T(8,128)S(1)} %bitcast.303), kind=kCustom, calls=%fused_computation.10 | custom fusion | flops 32768 | bytes 397312 | tf_op jit(solution)/shard_map/scatter-add | solution.py:124
  434.9 11.5 %collective-permute-start.8 = (f32[64,64,1]{1,2,0:T(1,128)S(1)}, f32[64,64,1]{1,2,0:T(1,128)S(1)}, u32[]{:S(2)}, u32[]{:S(2)}) collective-permute-start(f32[64,64,1]{1,2,0:T(1,128)S(1)} %get-tuple-element.356), channel_id=1, source_target_pairs={{0,1},{1,2},{2,3},{3,4},{4,5},{5,6},{6,7},{7,0},{8,9},{9,10},{10,1... | collective-permute-start | bytes 49160 | tf_op jit(solution)/shard_map/ppermute | solution.py:21
  446.4 3.4 copy.82
  453.1 15.2 %collective-permute-start.11 = (f32[1,64,130]{1,2,0:T(8,128)S(1)}, f32[1,64,130]{1,2,0:T(8,128)}, u32[]{:S(2)}, u32[]{:S(2)}) collective-permute-start(f32[1,64,130]{1,2,0:T(8,128)S(1)} %get-tuple-element.348), channel_id=1, source_target_pairs={{0,8},{8,16},{16,24},{1,9},{9,17},{17,25},{2,10},{10,18},{18,26},{... | collective-permute-start | bytes 99848 | tf_op jit(solution)/shard_map/ppermute | solution.py:21
  469.9 45.2 %while.52 = (s32[]{:T(128)}, f32[64,512]{1,0:T(8,128)S(1)}, f32[512,64]{0,1:T(8,128)}, f32[4,16,64,128]{3,2,1,0:T(8,128)}, bf16[4,16,64,128]{3,2,1,0:T(8,128)(2,...) while((s32[]{:T(128)}, f32[64,512]{1,0:T(8,128)S(1)}, ...), condition=%wide.region_14.15_spmd.clone, body=%wide.region_13.14_spmd.clone.sunk | while | flops 676462592 | bytes 46336196 | solution.py:97
  477.4 3.8 fusion.242
  488.7 3.8 fusion.242
  500.0 3.8 fusion.242
  511.3 3.8 fusion.242
  515.1 3.8 copy.83
  518.9 13.3 %fusion.121 = f32[64,64,128]{1,2,0:T(8,128)S(1)} fusion(f32[64,64,128]{1,2,0:T(8,128)} %scatter_fusion.3, f32[64,64,1]{1,2,0:T(1,128)S(1)} %collective-permute-done.8, f32[64,64,1]{1,2,0:T(1,128)S(1)} %collective-permute-done.9, f32[1,64,130]{1,2,0:T(8,128)} %collective-permute-done.11, f32[1,64,130]{1,2,0:T(8,128)} %collective-permute-done.10, ...), kind=kLoop, calls=%fused_computation.103 | loop fusion | flops 9437184 | bytes 6392064 | tf_op jit(solution)/shard_map/add | solution.py:181
  534.4 4.7 collective-permute-start.13
  539.1 3.4 copy.84
  545.3 3.7 collective-permute-start.15
  550.6 41.2 %while.53 = (s32[]{:T(128)}, f32[64,512]{1,0:T(8,128)S(1)}, f32[512,64]{0,1:T(8,128)}, f32[4,16,64,128]{3,2,1,0:T(8,128)}, bf16[4,16,64,128]{3,2,1,0:T(8,128)(2,...) while((s32[]{:T(128)}, f32[64,512]{1,0:T(8,128)S(1)}, ...), condition=%wide.region_16.17_spmd.clone, body=%wide.region_15.16_spmd.clone.sunk | while | flops 676462592 | bytes 37947028 | solution.py:97
  557.2 3.7 fusion.256
  567.5 3.7 fusion.256
  577.8 3.7 fusion.256
  588.1 3.7 fusion.256
  591.8 3.9 copy.85
  597.1 14.6 %fusion.112 = f32[64,64,128]{1,2,0:T(8,128)} fusion(f32[64,64,128]{1,2,0:T(8,128)} %copy-done.4, f32[64,64,1]{1,2,0:T(1,128)S(1)} %collective-permute-done.12, f32[64,64,1]{1,2,0:T(1,128)S(1)} %collective-permute-done.13, f32[1,64,130]{1,2,0:T(8,128)} %collective-permute-done.15, f32[1,64,130]{1,2,0:T(8,128)} %collective-permute-done.14, ...), kind=kLoop, calls=%fused_computation.86 | loop fusion | flops 9437184 | bytes 6392064 | tf_op jit(solution)/shard_map/add | solution.py:183
  611.7 3.8 copy.86
  615.5 108.1 %all-reduce.3.cloned.1.call-done = (f32[64,512]{1,0:T(8,128)}, f32[512,64]{0,1:T(8,128)}) async-done(((f32[64,512]{1,0:T(8,128)}, f32[512,64]{0,1:T(8,128)}), (f32[64,512]{1,0:T(8,128)}, f32[512,64]{0,1:T(8,128)})) %all-reduce.3.cloned.1.call-update) | async-done | bytes 262160 | tf_op jit(solution)/shard_map/psum | solution.py:184
  (198 shorter events, 117.3 us)
Async XLA Ops:
  7.2 174.3 %copy-start = (f32[128,64]{0,1:T(8,128)S(1)}, f32[128,64]{0,1:T(8,128)}, u32[]{:S(2)}) copy-start(f32[128,64]{0,1:T(8,128)} %param.22) | copy-start | bytes 98308
  7.2 17.7 %copy-start.10 = (f32[64,64,128]{2,1,0:T(8,128)S(1)}, f32[64,64,128]{2,1,0:T(8,128)}, u32[]{:S(2)}) copy-start(f32[64,64,128]{2,1,0:T(8,128)} %param.18) | copy-start | bytes 6291460
  7.2 11.2 %copy-start.22 = (s32[256,1]{0,1:T(1,128)S(1)}, s32[256,1]{0,1:T(1,128)}, u32[]{:S(2)}) copy-start(s32[256,1]{0,1:T(1,128)} %param.25) | copy-start | bytes 3076
  7.2 12.2 %copy-start.23 = (s32[256,4]{0,1:T(4,128)S(1)}, s32[256,4]{0,1:T(4,128)}, u32[]{:S(2)}) copy-start(s32[256,4]{0,1:T(4,128)} %param.26) | copy-start | bytes 12292
  11.1 14.2 %copy-start.7 = (bf16[64,512]{1,0:T(8,128)(2,1)S(1)}, bf16[64,512]{1,0:T(8,128)(2,1)}, u32[]{:S(2)}) copy-start(bf16[64,512]{1,0:T(8,128)(2,1)} %param.20) | copy-start | bytes 196612
  11.1 14.2 %copy-start.11 = (bf16[512,64]{0,1:T(8,128)(2,1)S(1)}, bf16[512,64]{0,1:T(8,128)(2,1)}, u32[]{:S(2)}) copy-start(bf16[512,64]{0,1:T(8,128)(2,1)} %param.21) | copy-start | bytes 196612
  12.3 21.6 %collective-permute-start = (f32[64,64,1]{1,2,0:T(1,128)S(1)}, f32[64,64,1]{1,2,0:T(1,128)S(1)}, u32[]{:S(2)}, u32[]{:S(2)}) collective-permute-start(f32[64,64,1]{1,2,0:T(1,128)S(1)} %get-tuple-element.359), channel_id=1, source_target_pairs={{0,1},{1,2},{2,3},{3,4},{4,5},{5,6},{6,7},{7,0},{8,9},{9,10},{10,1... | collective-permute-start | bytes 49160 | tf_op jit(solution)/shard_map/ppermute | solution.py:21
  15.3 18.5 %collective-permute-start.1 = (f32[64,64,1]{1,2,0:T(1,128)S(1)}, f32[64,64,1]{1,2,0:T(1,128)S(1)}, u32[]{:S(2)}, u32[]{:S(2)}) collective-permute-start(f32[64,64,1]{1,2,0:T(1,128)S(1)} %get-tuple-element.360), channel_id=1, source_target_pairs={{1,0},{2,1},{3,2},{4,3},{5,4},{6,5},{7,6},{0,7},{9,8},{10,9},{11,1... | collective-permute-start | bytes 49160 | tf_op jit(solution)/shard_map/ppermute | solution.py:22
  21.6 11.9 %all-to-all-start = ((s32[32,16,4]{1,2,0:T(4,128)}), s32[32,16,4]{1,2,0:T(4,128)S(1)}, u32[]{:S(2)}, u32[]{:S(2)}) async-start(s32[32,16,4]{1,2,0:T(4,128)} %copy.69), calls=%async_computation | async-start | bytes 131072 | tf_op jit(solution)/shard_map/all_to_all | solution.py:148
  25.4 5.4 copy-start.24
  30.8 48.0 %copy-start.16 = (f32[64]{0:T(128)}, f32[64]{0:T(128)S(1)}, u32[]{:S(2)}) copy-start(f32[64]{0:T(128)S(1)} %get-tuple-element.372) | copy-start | bytes 772
  30.8 48.0 %copy-start.19 = (f32[64]{0:T(128)}, f32[64]{0:T(128)S(1)}, u32[]{:S(2)}) copy-start(f32[64]{0:T(128)S(1)} %get-tuple-element.373) | copy-start | bytes 772
  33.8 7.7 %copy-start.6 = (f32[64,64,128]{1,2,0:T(8,128)S(1)}, f32[64,64,128]{1,2,0:T(8,128)}, u32[]{:S(2)}) copy-start(f32[64,64,128]{1,2,0:T(8,128)} %copy.71) | copy-start | bytes 6291460
  34.9 3.8 collective-permute-start.2
  37.2 4.3 collective-permute-start.3
  49.6 8.6 %collective-permute-start.4 = (f32[64,64,1]{1,2,0:T(1,128)S(1)}, f32[64,64,1]{1,2,0:T(1,128)S(1)}, u32[]{:S(2)}, u32[]{:S(2)}) collective-permute-start(f32[64,64,1]{1,2,0:T(1,128)S(1)} %get-tuple-element.357), channel_id=1, source_target_pairs={{0,1},{1,2},{2,3},{3,4},{4,5},{5,6},{6,7},{7,0},{8,9},{9,10},{10,1... | collective-permute-start | bytes 49160 | tf_op jit(solution)/shard_map/ppermute | solution.py:21
  51.1 7.1 collective-permute-start.5
  59.1 19.7 %collective-permute-start.6 = (f32[1,64,130]{1,2,0:T(8,128)S(1)}, f32[1,64,130]{1,2,0:T(8,128)S(1)}, u32[]{:S(2)}, u32[]{:S(2)}) collective-permute-start(f32[1,64,130]{1,2,0:T(8,128)S(1)} %get-tuple-element.349), channel_id=1, source_target_pairs={{0,8},{8,16},{16,24},{1,9},{9,17},{17,25},{2,10},{10,18},{18,26},{... | collective-permute-start | bytes 99848 | tf_op jit(solution)/shard_map/ppermute | solution.py:21
  63.4 15.3 %collective-permute-start.7 = (f32[1,64,130]{1,2,0:T(8,128)S(1)}, f32[1,64,130]{1,2,0:T(8,128)S(1)}, u32[]{:S(2)}, u32[]{:S(2)}) collective-permute-start(f32[1,64,130]{1,2,0:T(8,128)S(1)} %get-tuple-element.350), channel_id=1, source_target_pairs={{8,0},{16,8},{24,16},{9,1},{17,9},{25,17},{10,2},{18,10},{26,18},{... | collective-permute-start | bytes 99848 | tf_op jit(solution)/shard_map/ppermute | solution.py:22
  118.2 63.3 %copy-start.25 = (f32[256,128]{1,0:T(8,128)S(1)}, f32[256,128]{1,0:T(8,128)}, u32[]{:S(2)}) copy-start(f32[256,128]{1,0:T(8,128)} %param.24) | copy-start | bytes 393220
  118.3 63.3 %copy-start.26 = (s32[256]{0:T(256)S(1)}, s32[256]{0:T(256)}, u32[]{:S(2)}) copy-start(s32[256]{0:T(256)} %param.27) | copy-start | bytes 3076
  118.3 63.3 %copy-start.27 = (f32[128]{0:T(128)S(1)}, f32[128]{0:T(128)}, u32[]{:S(2)}) copy-start(f32[128]{0:T(128)} %param.23) | copy-start | bytes 1540
  148.9 30.3 %all-to-all-start.1 = ((f32[32,1,1024]{2,1,0:T(1,128)}), f32[32,1,1024]{2,1,0:T(1,128)S(1)}, u32[]{:S(2)}, u32[]{:S(2)}) async-start(f32[32,1,1024]{2,1,0:T(1,128)} %reshape.217), calls=%async_computation.1 | async-start | bytes 262144 | tf_op jit(solution)/shard_map/all_to_all | solution.py:160
  171.4 552.2 %all-reduce.3.cloned.1.call-start = ((), (), s32[]{:S(2)}) async-start(), calls=%async_computation.3 | async-start | bytes 524288 | tf_op jit(solution)/shard_map/psum | solution.py:184
  434.9 14.9 %collective-permute-start.8 = (f32[64,64,1]{1,2,0:T(1,128)S(1)}, f32[64,64,1]{1,2,0:T(1,128)S(1)}, u32[]{:S(2)}, u32[]{:S(2)}) collective-permute-start(f32[64,64,1]{1,2,0:T(1,128)S(1)} %get-tuple-element.356), channel_id=1, source_target_pairs={{0,1},{1,2},{2,3},{3,4},{4,5},{5,6},{6,7},{7,0},{8,9},{9,10},{10,1... | collective-permute-start | bytes 49160 | tf_op jit(solution)/shard_map/ppermute | solution.py:21
  446.4 3.9 collective-permute-start.9
  451.9 67.1 %collective-permute-start.10 = (f32[1,64,130]{1,2,0:T(8,128)}, f32[1,64,130]{1,2,0:T(8,128)}, u32[]{:S(2)}, u32[]{:S(2)}) collective-permute-start(f32[1,64,130]{1,2,0:T(8,128)} %get-tuple-element.347), channel_id=1, source_target_pairs={{8,0},{16,8},{24,16},{9,1},{17,9},{25,17},{10,2},{18,10},{26,18},{... | collective-permute-start | bytes 99848 | tf_op jit(solution)/shard_map/ppermute | solution.py:22
  453.1 65.8 %collective-permute-start.11 = (f32[1,64,130]{1,2,0:T(8,128)S(1)}, f32[1,64,130]{1,2,0:T(8,128)}, u32[]{:S(2)}, u32[]{:S(2)}) collective-permute-start(f32[1,64,130]{1,2,0:T(8,128)S(1)} %get-tuple-element.348), channel_id=1, source_target_pairs={{0,8},{8,16},{16,24},{1,9},{9,17},{17,25},{2,10},{10,18},{18,26},{... | collective-permute-start | bytes 99848 | tf_op jit(solution)/shard_map/ppermute | solution.py:21
  477.4 3.8 copy-start.9
  488.7 3.8 copy-start.9
  500.0 3.8 copy-start.9
  511.3 3.8 copy-start.9
  515.1 17.2 %copy-start.13 = (f32[64,512]{1,0:T(8,128)}, f32[64,512]{1,0:T(8,128)S(1)}, u32[]{:S(2)}) copy-start(f32[64,512]{1,0:T(8,128)S(1)} %get-tuple-element.150) | copy-start | bytes 393220
  515.1 3.9 copy-start.17
  515.1 3.9 copy-start.20
  534.3 8.2 %collective-permute-start.12 = (f32[64,64,1]{1,2,0:T(1,128)S(1)}, f32[64,64,1]{1,2,0:T(1,128)S(1)}, u32[]{:S(2)}, u32[]{:S(2)}) collective-permute-start(f32[64,64,1]{1,2,0:T(1,128)S(1)} %get-tuple-element.354), channel_id=1, source_target_pairs={{0,1},{1,2},{2,3},{3,4},{4,5},{5,6},{6,7},{7,0},{8,9},{9,10},{10,1... | collective-permute-start | bytes 49160 | tf_op jit(solution)/shard_map/ppermute | solution.py:21
  534.4 8.1 %collective-permute-start.13 = (f32[64,64,1]{1,2,0:T(1,128)S(1)}, f32[64,64,1]{1,2,0:T(1,128)S(1)}, u32[]{:S(2)}, u32[]{:S(2)}) collective-permute-start(f32[64,64,1]{1,2,0:T(1,128)S(1)} %get-tuple-element.353), channel_id=1, source_target_pairs={{1,0},{2,1},{3,2},{4,3},{5,4},{6,5},{7,6},{0,7},{9,8},{10,9},{11,1... | collective-permute-start | bytes 49160 | tf_op jit(solution)/shard_map/ppermute | solution.py:22
  544.0 53.0 %collective-permute-start.14 = (f32[1,64,130]{1,2,0:T(8,128)}, f32[1,64,130]{1,2,0:T(8,128)}, u32[]{:S(2)}, u32[]{:S(2)}) collective-permute-start(f32[1,64,130]{1,2,0:T(8,128)} %get-tuple-element.345), channel_id=1, source_target_pairs={{8,0},{16,8},{24,16},{9,1},{17,9},{25,17},{10,2},{18,10},{26,18},{... | collective-permute-start | bytes 99848 | tf_op jit(solution)/shard_map/ppermute | solution.py:22
  545.3 51.8 %collective-permute-start.15 = (f32[1,64,130]{1,2,0:T(8,128)}, f32[1,64,130]{1,2,0:T(8,128)}, u32[]{:S(2)}, u32[]{:S(2)}) collective-permute-start(f32[1,64,130]{1,2,0:T(8,128)} %get-tuple-element.346), channel_id=1, source_target_pairs={{0,8},{8,16},{16,24},{1,9},{9,17},{17,25},{2,10},{10,18},{18,26},{... | collective-permute-start | bytes 99848 | tf_op jit(solution)/shard_map/ppermute | solution.py:21
  551.4 2.0 copy-start.3
  561.6 2.0 copy-start.3
  571.9 2.0 copy-start.3
  591.8 3.9 copy-start.12
  591.8 3.9 copy-start.15
  591.8 4.6 copy-start.14
  591.8 5.3 copy-start.18
  591.8 5.3 copy-start.21
  597.1 129.7 %copy-start.1 = (f32[128,64]{0,1:T(8,128)S(1)}, f32[128,64]{0,1:T(8,128)}, u32[]{:S(2)}) copy-start(f32[128,64]{0,1:T(8,128)} %param.22) | copy-start | bytes 98308
  (12 other events, 18.2 us)
Sparse Core Ops, SparseCore 0:
  597.2 126.4 all-reduce.2
where the time goes:
time: 741 us; the launch traced here: 734 us
  other arithmetic  300 us (40%)
  local copies, waits for them, and re-layouts  121 us (16%)
  waiting for transfers between devices  119 us (16%)
  matrix products  84.7 us (11%)
  starting transfers between devices  83.8 us (11%)
  between operations  14.6 us (2%)
  blocking collectives  9.97 us (1%)
    scatter-add x4, other arithmetic, spread_back(): adjoint_two.at[cell_rows[:, corner], :, cell_cols[:, corner]]  234 us
    psum x1, waiting for transfers between devices, on_device(): lax.psum((gin_one + gin_zero, gout_one + gout_zero), ('lat', 'lon'))  108 us
    ppermute x8, starting transfers between devices, padded(): before = lax.ppermute(last, axis, up)  41.6 us
    gather x3, local copies, waits for them, and re-layouts, interpolate(): state_two[cell_rows[:, corner], :, cell_cols[:, corner]]  39.5 us
    dot_general x8, matrix products, one_block(): jnp.einsum('ghw,gfw->hf', hidden, cot_low, preferred_element_type=jnp.flo...  30 us
    all_to_all x1, starting transfers between devices, on_device(): lax.all_to_all(slot_interp, ('lat', 'lon'), split_axis=0, concat_axis=0,...  22.5 us
    unnamed x59, local copies, waits for them, and re-layouts  22.1 us
    ppermute x8, starting transfers between devices, padded(): after = lax.ppermute(initial, axis, down)  16.4 us
  transfers between devices with their start and end apart: 19, of which 4 were waited for; matrix products, arithmetic and copies ran while one was open for 19% of the time, Pallas kernels for 0%

commit v1 on v0

v1 whole, which is shorter than its diff:
```python
import functools
import math

import jax
import jax.numpy as jnp
from jax import lax
from jax.experimental import pallas as pl
from jax.experimental.pallas import tpu as pltpu
from jax.sharding import PartitionSpec as P

CAP = 16
GROUP = 4
VMEM_LIMIT = 48 * 1024 * 1024
corner_tenths = (4, 3, 2, 1)
TENTH = 0.1


def fill_rows(rows, x_ref, north_ref, south_ref):
    count = x_ref.shape[0]
    rows[pl.ds(1, count)] = x_ref[...]
    rows[0] = north_ref[...]
    rows[count + 1] = south_ref[...]


def stencil_row(rows, left, right, weights, i):
    count, (feat, width) = rows.shape[0] - 2, rows.shape[1:]
    lane = lax.broadcasted_iota(jnp.int32, (feat, width), 1)
    here = rows[i + 1]
    west = jnp.where(
        lane == 0, pltpu.roll(left, width - count - i, axis=1), pltpu.roll(here, 1, axis=1)
    )
    east = jnp.where(
        lane == width - 1,
        pltpu.roll(right, width - 1 - i, axis=1),
        pltpu.roll(here, width - 1, axis=1),
    )
    return (
        weights[0] * here
        + weights[1] * rows[i]
        + weights[2] * rows[i + 2]
        + weights[3] * west
        + weights[4] * east
    )


def keep_edges(edge_ref, row, i, count):
    feat, width = row.shape
    lane = lax.broadcasted_iota(jnp.int32, (feat, width), 1)
    edge_ref[...] = jnp.where(
        lane == i,
        pltpu.roll(row, i, axis=1),
        jnp.where(
            lane == count + i,
            pltpu.roll(row, lax.rem(count + i + 1, width), axis=1),
            edge_ref[...],
        ),
    )


def weights_of(c_ref, order, width):
    feat = c_ref.shape[0]
    return [jnp.broadcast_to(c_ref[:, k : k + 1], (feat, width)) for k in order]


def mm(a, b):
    return jnp.dot(a, b, preferred_element_type=jnp.float32)


def mm_nt(a, b):
    return lax.dot_general(a, b, (((1,), (1,)), ((), ())), preferred_element_type=jnp.float32)


def two_parts(x):
    high = x.astype(jnp.bfloat16)
    low = (x - high.astype(jnp.float32)).astype(jnp.bfloat16)
    return jnp.concatenate([high, low], axis=0)


def forward_group(rows, left, right, weights, wit_ref, wot_ref, base):
    width = rows.shape[2]
    inputs = jnp.concatenate([rows[base + g + 1] for g in range(GROUP)], axis=1).astype(
        jnp.bfloat16
    )
    hidden = jnp.tanh(mm(wit_ref[...], inputs)).astype(jnp.bfloat16)
    closure = mm(wot_ref[...], hidden)
    return [
        stencil_row(rows, left, right, weights, base + g) + closure[:, g * width : (g + 1) * width]
        for g in range(GROUP)
    ]


def forward_kernel(
    x_ref, n_ref, s_ref, l_ref, r_ref, c_ref, wit_ref, wot_ref, o_ref, edge_ref, rows
):
    count, feat, width = x_ref.shape
    fill_rows(rows, x_ref, n_ref, s_ref)
    edge_ref[...] = jnp.zeros_like(edge_ref)

    def step(b, carry):
        base = b * GROUP
        weights = weights_of(c_ref, (0, 1, 2, 3, 4), width)
        out = forward_group(
            rows, l_ref[...], r_ref[...], weights, wit_ref, wot_ref, base
        )
        for g in range(GROUP):
            o_ref[base + g] = out[g]
            keep_edges(edge_ref, out[g], base + g, count)
        return carry

    lax.fori_loop(0, count // GROUP, step, 0)


def forward_interp_kernel(
    x_ref, n_ref, s_ref, l_ref, r_ref, c_ref, wit_ref, wot_ref, cell_ref, o_ref, rows, acc
):
    count, feat, width = x_ref.shape
    slots = cell_ref.shape[1]
    block = min(slots, 512)
    fill_rows(rows, x_ref, n_ref, s_ref)
    acc[...] = jnp.zeros_like(acc)

    def step(b, carry):
        base = b * GROUP
        weights = weights_of(c_ref, (0, 1, 2, 3, 4), width)
        out = forward_group(
            rows, l_ref[...], r_ref[...], weights, wit_ref, wot_ref, base
        )
        parts = two_parts(jnp.concatenate(out, axis=1))
        for s in range(0, slots, block):
            cell = (
                lax.broadcasted_iota(jnp.int32, (GROUP * width, block), 0) + base * width
            )
            pick = jnp.zeros((GROUP * width, block), jnp.float32)
            for k in range(4):
                pick = pick + jnp.where(
                    cell == cell_ref[k : k + 1, s : s + block], float(corner_tenths[k]), 0.0
                )
            both = mm(parts, pick.astype(jnp.bfloat16))
            acc[:, s : s + block] += both[:feat] + both[feat:]
        return carry

    lax.fori_loop(0, count // GROUP, step, 0)
    o_ref[...] = jnp.transpose(acc[...] * TENTH)


def spread_kernel(pulled_ref, cell_ref, o_ref, edge_ref, parts):
    count, feat, width = o_ref.shape
    slots = cell_ref.shape[0]
    edge_ref[...] = jnp.zeros_like(edge_ref)
    parts[...] = two_parts(jnp.transpose(pulled_ref[...]) * TENTH)
    block = min(slots, 512)

    def step(b, carry):
        base = b * GROUP
        total = jnp.zeros((2 * feat, GROUP * width), jnp.float32)
        for s in range(0, slots, block):
            cell = (
                lax.broadcasted_iota(jnp.int32, (block, GROUP * width), 1) + base * width
            )
            pick = jnp.zeros((block, GROUP * width), jnp.float32)
            for k in range(4):
                pick = pick + jnp.where(
                    cell == cell_ref[s : s + block, k : k + 1], float(corner_tenths[k]), 0.0
                )
            total = total + mm(parts[:, s : s + block], pick.astype(jnp.bfloat16))
        out = total[:feat] + total[feat:]
        for g in range(GROUP):
            row = out[:, g * width : (g + 1) * width]
            o_ref[base + g] = row
            keep_edges(edge_ref, row, base + g, count)
        return carry

    lax.fori_loop(0, count // GROUP, step, 0)


def backward_kernel(
    v_ref,
    x_ref,
    n_ref,
    s_ref,
    l_ref,
    r_ref,
    c_ref,
    wit_ref,
    wi_ref,
    wo_ref,
    o_ref,
    edge_ref,
    grad_ref,
    rows,
    gin,
    gout,
):
    count, feat, width = x_ref.shape
    fill_rows(rows, x_ref, n_ref, s_ref)
    edge_ref[...] = jnp.zeros_like(edge_ref)
    gin[...] = jnp.zeros_like(gin)
    gout[...] = jnp.zeros_like(gout)

    def step(b, carry):
        base = b * GROUP
        weights = weights_of(c_ref, (0, 2, 1, 4, 3), width)
        inputs = jnp.concatenate([v_ref[base + g] for g in range(GROUP)], axis=1).astype(
            jnp.bfloat16
        )
        cot = jnp.concatenate([rows[base + g + 1] for g in range(GROUP)], axis=1).astype(
            jnp.bfloat16
        )
        tanh_pre = jnp.tanh(mm(wit_ref[...], inputs))
        hidden = tanh_pre.astype(jnp.bfloat16)
        gout[...] += mm_nt(hidden, cot)
        back_hidden = mm(wo_ref[...], cot)
        back_pre = (back_hidden * (1.0 - tanh_pre * tanh_pre)).astype(jnp.bfloat16)
        gin[...] += mm_nt(back_pre, inputs)
        back = mm(wi_ref[...], back_pre)
        for g in range(GROUP):
            row = (
                stencil_row(rows, l_ref[...], r_ref[...], weights, base + g)
                + back[:, g * width : (g + 1) * width]
            )
            o_ref[base + g] = row
            keep_edges(edge_ref, row, base + g, count)
        return carry

    lax.fori_loop(0, count // GROUP, step, 0)
    grad_ref[...] = jnp.concatenate([gin[...], gout[...]], axis=1)


def call(kernel, outs, scratch, *args):
    return pl.pallas_call(
        kernel,
        out_shape=outs,
        in_specs=[pl.BlockSpec(memory_space=pltpu.VMEM)] * len(args),
        out_specs=jax.tree.map(lambda _: pl.BlockSpec(memory_space=pltpu.VMEM), outs),
        scratch_shapes=scratch,
        compiler_params=pltpu.CompilerParams(vmem_limit_bytes=VMEM_LIMIT),
    )(*args)


def halos(field, edges):
    lat, lon = lax.axis_size("lat"), lax.axis_size("lon")
    south = [(i, i + 1) for i in range(lat - 1)]
    north = [(i + 1, i) for i in range(lat - 1)]
    east = [(i, (i + 1) % lon) for i in range(lon)]
    west = [((i + 1) % lon, i) for i in range(lon)]
    return (
        lax.ppermute(field[-1], "lat", south),
        lax.ppermute(field[0], "lat", north),
        lax.ppermute(edges, "lon", east),
        lax.ppermute(edges, "lon", west),
    )


def swap(blocks):
    return lax.all_to_all(blocks, ("lat", "lon"), split_axis=0, concat_axis=0, tiled=True)


def f32(*shape):
    return jax.ShapeDtypeStruct(shape, jnp.float32)


def on_device(
    start_state, coefficients, w_in, w_out, jacobian, sigma, obs_values, owner, stencil, counts
):
    tlat, feat, tlon = start_state.shape
    hid = w_in.shape[1]
    lat_count = lax.axis_size("lat")
    lon_count = lax.axis_size("lon")
    devices = lat_count * lon_count
    channels = obs_values.shape[1]
    slots = devices * CAP
    rows_scratch = pltpu.VMEM((tlat + 2, feat, tlon), jnp.float32)
    tile, edge_shape = f32(tlat, feat, tlon), f32(feat, tlon)

    tile_owner = owner[:, 0]
    onehot = (tile_owner[:, None] == jnp.arange(devices, dtype=jnp.int32)[None, :]).astype(
        jnp.int32
    )
    running = jnp.cumsum(onehot, axis=0)
    rank = jnp.sum(running * onehot, axis=1) - 1
    slot = tile_owner * CAP + rank
    send_stencil = jnp.zeros((slots, 4), jnp.int32).at[slot].set(stencil)
    cell_recv = swap(send_stencil)

    coef = coefficients.T
    w_in_t, w_out_t = w_in.T, w_out.T
    start_edges = jnp.concatenate([start_state[:, :, 0].T, start_state[:, :, -1].T], axis=1)
    state_one, edges_one = call(
        forward_kernel,
        (tile, edge_shape),
        [rows_scratch],
        start_state,
        *halos(start_state, start_edges),
        coef,
        w_in_t,
        w_out_t,
    )
    slot_interp = call(
        forward_interp_kernel,
        f32(slots, feat),
        [rows_scratch, pltpu.VMEM((feat, slots), jnp.float32)],
        state_one,
        *halos(state_one, edges_one),
        coef,
        w_in_t,
        w_out_t,
        cell_recv.T,
    )
    row_interp = swap(slot_interp)[slot]
    evolved = jnp.dot(
        row_interp, jacobian.T, precision=lax.Precision.HIGHEST, preferred_element_type=jnp.float32
    )
    used = jnp.arange(channels, dtype=jnp.int32)[None, :] < counts[:, None]
    departures = jnp.where(used, (obs_values - evolved) / sigma[None, :], 0.0)
    row_pulled = jnp.dot(
        -departures / sigma[None, :],
        jacobian,
        precision=lax.Precision.HIGHEST,
        preferred_element_type=jnp.float32,
    )
    recv_pulled = swap(jnp.zeros((slots, feat), jnp.float32).at[slot].set(row_pulled))
    adjoint_two, edges_two = call(
        spread_kernel,
        (tile, edge_shape),
        [pltpu.VMEM((2 * feat, slots), jnp.bfloat16)],
        recv_pulled,
        cell_recv,
    )

    def backward(state, cotangent, edges):
        return call(
            backward_kernel,
            (tile, edge_shape, f32(hid, 2 * feat)),
            [rows_scratch] + [pltpu.VMEM((hid, feat), jnp.float32)] * 2,
            state,
            cotangent,
            *halos(cotangent, edges),
            coef,
            w_in_t,
            w_in,
            w_out,
        )

    adjoint_one, edges_adj, grads_one = backward(state_one, adjoint_two, edges_two)
    grad_state, _, grads_zero = backward(start_state, adjoint_one, edges_adj)
    grads = (grads_one + grads_zero).reshape(devices, hid // devices, 2 * feat)
    part = jnp.sum(swap(grads), axis=0)
    scale = 1.0 / math.sqrt(tlat * lat_count * tlon * lon_count)
    part = part * scale
    total = swap(jnp.broadcast_to(part[None], grads.shape)).reshape(hid, 2 * feat)
    return (grad_state, departures, total[:, :feat].T, total[:, feat:])


def solution(mesh):
    return jax.shard_map(
        on_device,
        mesh=mesh,
        in_specs=(
            P("lat", None, "lon"),
            P(),
            P(),
            P(),
            P(),
            P(),
            P(("lat", "lon"), None),
            P(("lat", "lon"), None),
            P(("lat", "lon"), None),
            P(("lat", "lon")),
        ),
        out_specs=(P("lat", None, "lon"), P(("lat", "lon"), None), P(), P()),
        check_vma=False,
    )
```

time: 741 us -> 200 us (0.27)
  other arithmetic: 300 us -> 2.79 us
  waiting for transfers between devices: 119 us -> 13.1 us
  local copies, waits for them, and re-layouts: 121 us -> 22.9 us
  matrix products: 84.7 us -> 0.51 us
  Pallas kernels: 0 us -> 68 us
  starting transfers between devices: 83.8 us -> 35.4 us
  blocking collectives: 9.97 us -> 55.3 us
  between operations: 14.6 us -> 1.11 us
    scatter-add x4 -> x0, other arithmetic: 234 us -> none  [spread_back(): adjoint_two.at[cell_rows[:, corner], :, cell_cols[:, corner]]]
    psum x1 -> x0, waiting for transfers between devices: 108 us -> none  [on_device(): lax.psum((gin_one + gin_zero, gout_one + gout_zero), ('lat', 'lon'))]
    dot_general x48 -> x0, matrix products: 84.2 us -> none  [the longest x8 30 us: one_block(): jnp.einsum('ghw,gfw->hf', hidden, cot_low, preferred_element_type=jnp.flo...]
    pallas_call x0 -> x5, Pallas kernels: none -> 68 us  [call(): pl.pallas_call(kernel, out_shape=outs, in_specs=[pl.BlockSpec(memory_spac...]
    add x7 -> x1, other arithmetic: 51.9 us -> 0.03 us  [on_device(): grads = (grads_one + grads_zero).reshape(devices, hid // devices, 2 * feat)]
    gather x5 -> x1, local copies, waits for them, and re-layouts: 52.5 us -> 0.73 us  [on_device(): row_interp = swap(slot_interp)[slot]]
    all_to_all x1 -> x4, blocking collectives: 9.97 us -> 55.3 us  [swap(): lax.all_to_all(blocks, ('lat', 'lon'), split_axis=0, concat_axis=0, tiled...]
    while x37 -> x0, local copies, waits for them, and re-layouts: 32.5 us -> none
  transfers between devices with their start and end apart: 19 -> 17, of which waited for: 4 -> 4; matrix products, arithmetic and copies ran while one was open for 19% -> 2% of each run, Pallas kernels for 0% -> 0%
where the time goes in v1:
time: 200 us; the launch traced here: 199 us
  Pallas kernels  68 us (34%)
  blocking collectives  55.3 us (28%)
  starting transfers between devices  35.4 us (18%)
  local copies, waits for them, and re-layouts  22.9 us (11%)
  waiting for transfers between devices  13.1 us (7%)
  other arithmetic  2.79 us (1%)
    pallas_call x5, Pallas kernels, call(): pl.pallas_call(kernel, out_shape=outs, in_specs=[pl.BlockSpec(memory_spac...  68 us
    all_to_all x4, blocking collectives, swap(): lax.all_to_all(blocks, ('lat', 'lon'), split_axis=0, concat_axis=0, tiled...  55.3 us
    ppermute x4, starting transfers between devices, halos(): lax.ppermute(edges, 'lon', west)  15.1 us
    unnamed x42, local copies, waits for them, and re-layouts  13.2 us
    ppermute x4, starting transfers between devices, halos(): lax.ppermute(field[-1], 'lat', south)  12.5 us
    all_to_all x1, waiting for transfers between devices, swap(): lax.all_to_all(blocks, ('lat', 'lon'), split_axis=0, concat_axis=0, tiled...  7.79 us
    ppermute x4, waiting for transfers between devices, halos(): lax.ppermute(edges, 'lon', east)  5.32 us
    ppermute x4, starting transfers between devices, halos(): lax.ppermute(field[0], 'lat', north)  5.16 us
  transfers between devices with their start and end apart: 17, of which 4 were waited for; matrix products, arithmetic and copies ran while one was open for 2% of the time, Pallas kernels for 0%

profile of v1, /device:TPU:0, one launch (start us, length us, event | category | flops | bytes accessed | tf_op | source)
XLA Modules:
  0.0 199.1 jit_solution(8063412391372959847)
XLA Ops:
  0.6 5.0 %fusion.13 = (f32[64,64,1]{2,1,0:T(8,128)}, f32[64,64,1]{2,1,0:T(8,128)}) fusion(f32[64,64,128]{2,1,0:T(8,128)} %v_ref.1), kind=kLoop, calls=%fused_computation.37 | loop fusion | bytes 65536 | tf_op jit(solution)/shard_map/slice | solution.py:287
  5.7 2.8 %copy.48 = f32[64,64,1]{0,1,2:T(8,128)S(1)} copy(f32[64,64,1]{2,1,0:T(8,128)} %get-tuple-element.36) | data formatting | bytes 32768
  8.5 2.6 %copy.49 = f32[64,64,1]{0,1,2:T(8,128)S(1)} copy(f32[64,64,1]{2,1,0:T(8,128)} %get-tuple-element.37) | data formatting | bytes 32768
  11.2 6.0 %collective-permute-start.3 = (f32[64,128]{1,0:T(8,128)S(1)}, f32[64,128]{1,0:T(8,128)S(1)}, u32[]{:S(2)}, u32[]{:S(2)}) collective-permute-start(f32[64,128]{1,0:T(8,128)S(1)} %pad_maximum_fusion), channel_id=1, source_target_pairs={{1,0},{2,1},{3,2},{4,3},{5,4},{6,5},{7,6},{0,7},{9,8},{10,9},{11,1... | collective-permute-start | bytes 98312 | tf_op jit(solution)/shard_map/ppermute | solution.py:250
  17.2 1.3 collective-permute-start.1
  18.5 3.0 %collective-permute-start = (f32[64,128]{1,0:T(8,128)S(1)}, f32[64,128]{1,0:T(8,128)S(1)}, u32[]{:S(2)}, u32[]{:S(2)}) collective-permute-start(f32[64,128]{1,0:T(8,128)S(1)} %get-tuple-element.39), channel_id=1, source_target_pairs={{0,8},{8,16},{16,24},{1,9},{9,17},{17,25},{2,10},{10,18},{18,26},{... | collective-permute-start | bytes 98312 | tf_op jit(solution)/shard_map/ppermute | solution.py:247
  21.6 0.6 reduce-window.6
  22.2 0.2 slice_reduce_fusion
  22.8 1.0 collective-permute-done.2.l_ref
  23.8 9.4 %shard_map.129 = (f32[64,64,128]{2,1,0:T(8,128)S(1)}, f32[64,128]{1,0:T(8,128)S(1)}) custom-call(f32[64,64,128]{2,1,0:T(8,128)S(1)} %copy-done.1, f32[64,128]{1,0:T(8,128)S(1)} %collective-permute-done.n_ref, f32[64,128]{1,0:T(8,128)S(1)} %collective-permute-done.1.s_ref, f32[64,128]{1,0:T(8,128)S(1)} %collective-permute-done.2.l_ref, ...), custom_call_target="tpu_custom_call" | custom-call | tf_op jit(solution)/shard_map/pallas_call | solution.py:230
  33.2 3.8 %collective-permute-start.7 = (f32[64,128]{1,0:T(8,128)S(1)}, f32[64,128]{1,0:T(8,128)S(1)}, u32[]{:S(2)}, u32[]{:S(2)}) collective-permute-start(f32[64,128]{1,0:T(8,128)S(1)} %get-tuple-element.14), channel_id=1, source_target_pairs={{1,0},{2,1},{3,2},{4,3},{5,4},{6,5},{7,6},{0,7},{9,8},{10,9},{11,1... | collective-permute-start | bytes 98312 | tf_op jit(solution)/shard_map/ppermute | solution.py:250
  37.0 1.3 copy-done.2
  38.3 1.3 collective-permute-start.5
  39.6 3.4 %collective-permute-start.4 = (f32[64,128]{1,0:T(8,128)S(1)}, f32[64,128]{1,0:T(8,128)S(1)}, u32[]{:S(2)}, u32[]{:S(2)}) collective-permute-start(f32[64,128]{1,0:T(8,128)S(1)} %get-tuple-element.35), channel_id=1, source_target_pairs={{0,8},{8,16},{16,24},{1,9},{9,17},{17,25},{2,10},{10,18},{18,26},{... | collective-permute-start | bytes 98312 | tf_op jit(solution)/shard_map/ppermute | solution.py:247
  43.1 1.2 scatter_custom_fusion
  44.4 0.2 copy.39
  44.6 14.4 %all_to_all.44 = s32[32,16,4]{1,2,0:T(4,128)S(1)} all-to-all(s32[32,16,4]{1,2,0:T(4,128)S(1)} %copy.39), channel_id=1, replica_groups=mesh['lat'=4,'lon'=8] {'lat','lon'}, dimensions={0} | all-to-all | bytes 16384 | tf_op jit(solution)/shard_map/all_to_all | solution.py:255
  59.0 0.3 copy.40
  59.4 1.6 copy-done.3
  61.0 15.3 %shard_map.130 = f32[512,64]{1,0:T(8,128)S(1)} custom-call(f32[64,64,128]{2,1,0:T(8,128)S(1)} %copy-done.3, f32[64,128]{1,0:T(8,128)S(1)} %collective-permute-done.4.n_ref, f32[64,128]{1,0:T(8,128)S(1)} %collective-permute-done.5.s_ref, f32[64,128]{1,0:T(8,128)S(1)} %collective-permute-done.6.l_ref, f32[64,128]{1,0:T(8,128)S(1)} %collective-permute-done.7.r_ref, ...), custom_call_target="tpu_custom_call" | custom-call | tf_op jit(solution)/shard_map/pallas_call | solution.py:230
  76.3 0.8 reshape.82
  77.1 2.6 %all-to-all-start.1 = ((f32[32,1,1024]{2,1,0:T(1,128)}), f32[32,1,1024]{2,1,0:T(1,128)S(1)}, u32[]{:S(2)}, u32[]{:S(2)}) async-start(f32[32,1,1024]{2,1,0:T(1,128)} %reshape.82), calls=%async_computation.1 | async-start | bytes 262144 | tf_op jit(solution)/shard_map/all_to_all | solution.py:255
  79.7 7.8 %all-to-all-done.1 = f32[32,1,1024]{2,1,0:T(1,128)S(1)} async-done(((f32[32,1,1024]{2,1,0:T(1,128)}), f32[32,1,1024]{2,1,0:T(1,128)S(1)}, u32[]{:S(2)}, u32[]{:S(2)}) %all-to-all-start.1) | async-done | bytes 131104 | tf_op jit(solution)/shard_map/all_to_all | solution.py:255
  87.5 0.5 broadcast.57
  88.0 0.9 reduce.2
  89.1 0.7 gather_fusion
  89.9 0.3 fusion.1
  90.1 0.3 fusion.2
  90.4 1.2 scatter_custom_fusion.1
  91.6 0.2 reshape.84
  91.8 9.9 %all_to_all.45 = f32[32,1,1024]{2,1,0:T(1,128)S(1)} all-to-all(f32[32,1,1024]{2,1,0:T(1,128)S(1)} %reshape.84), channel_id=1, replica_groups=mesh['lat'=4,'lon'=8] {'lat','lon'}, dimensions={0} | all-to-all | bytes 262144 | tf_op jit(solution)/shard_map/all_to_all | solution.py:255
  101.7 1.0 reduce.3
  102.8 12.4 %shard_map.131 = (f32[64,64,128]{2,1,0:T(8,128)S(1)}, f32[64,128]{1,0:T(8,128)S(1)}) custom-call(f32[512,64]{1,0:T(8,128)S(1)} %bitcast.67, s32[512,4]{1,0:T(8,128)S(1)} %bitcast.66), custom_call_target="tpu_custom_call" | custom-call | tf_op jit(solution)/shard_map/pallas_call | solution.py:230
  115.2 2.0 %collective-permute-start.11 = (f32[64,128]{1,0:T(8,128)S(1)}, f32[64,128]{1,0:T(8,128)S(1)}, u32[]{:S(2)}, u32[]{:S(2)}) collective-permute-start(f32[64,128]{1,0:T(8,128)S(1)} %get-tuple-element.16), channel_id=1, source_target_pairs={{1,0},{2,1},{3,2},{4,3},{5,4},{6,5},{7,6},{0,7},{9,8},{10,9},{11,1... | collective-permute-start | bytes 98312 | tf_op jit(solution)/shard_map/ppermute | solution.py:250
  117.3 1.3 collective-permute-start.9
  118.6 3.0 %collective-permute-start.8 = (f32[64,128]{1,0:T(8,128)S(1)}, f32[64,128]{1,0:T(8,128)S(1)}, u32[]{:S(2)}, u32[]{:S(2)}) collective-permute-start(f32[64,128]{1,0:T(8,128)S(1)} %get-tuple-element.33), channel_id=1, source_target_pairs={{0,8},{8,16},{16,24},{1,9},{9,17},{17,25},{2,10},{10,18},{18,26},{... | collective-permute-start | bytes 98312 | tf_op jit(solution)/shard_map/ppermute | solution.py:247
  121.7 2.0 %collective-permute-done.10.l_ref = f32[64,128]{1,0:T(8,128)S(1)} collective-permute-done((f32[64,128]{1,0:T(8,128)S(1)}, f32[64,128]{1,0:T(8,128)S(1)}, u32[]{:S(2)}, u32[]{:S(2)}) %collective-permute-start.10) | collective-permute-done | bytes 32800 | tf_op jit(solution)/shard_map/ppermute | solution.py:249
  123.8 1.6 copy-done.4
  125.4 15.7 %shard_map.132 = (f32[64,64,128]{2,1,0:T(8,128)S(1)}, f32[64,128]{1,0:T(8,128)S(1)}, f32[512,128]{1,0:T(8,128)S(1)}) custom-call(f32[64,64,128]{2,1,0:T(8,128)S(1)} %copy-done.4, f32[64,64,128]{2,1,0:T(8,128)} %copy-done.5, f32[64,128]{1,0:T(8,128)S(1)} %collective-permute-done.8.n_ref, f32[64,128]{1,0:T(8,128)S(1)} %collective-permute-done.9.s_ref, ...), custom_call_target="tpu_custom_call" | custom-call | tf_op jit(solution)/shard_map/pallas_call | solution.py:230
  141.1 3.3 %collective-permute-start.15 = (f32[64,128]{1,0:T(8,128)S(1)}, f32[64,128]{1,0:T(8,128)S(1)}, u32[]{:S(2)}, u32[]{:S(2)}) collective-permute-start(f32[64,128]{1,0:T(8,128)S(1)} %get-tuple-element.18), channel_id=1, source_target_pairs={{1,0},{2,1},{3,2},{4,3},{5,4},{6,5},{7,6},{0,7},{9,8},{10,9},{11,1... | collective-permute-start | bytes 98312 | tf_op jit(solution)/shard_map/ppermute | solution.py:250
  144.5 1.3 collective-permute-start.13
  145.8 3.0 %collective-permute-start.12 = (f32[64,128]{1,0:T(8,128)S(1)}, f32[64,128]{1,0:T(8,128)S(1)}, u32[]{:S(2)}, u32[]{:S(2)}) collective-permute-start(f32[64,128]{1,0:T(8,128)S(1)} %get-tuple-element.31), channel_id=1, source_target_pairs={{0,8},{8,16},{16,24},{1,9},{9,17},{17,25},{2,10},{10,18},{18,26},{... | collective-permute-start | bytes 98312 | tf_op jit(solution)/shard_map/ppermute | solution.py:247
  148.8 2.2 %collective-permute-done.14.l_ref = f32[64,128]{1,0:T(8,128)S(1)} collective-permute-done((f32[64,128]{1,0:T(8,128)S(1)}, f32[64,128]{1,0:T(8,128)S(1)}, u32[]{:S(2)}, u32[]{:S(2)}) %collective-permute-start.14) | collective-permute-done | bytes 32800 | tf_op jit(solution)/shard_map/ppermute | solution.py:249
  151.1 15.2 %shard_map.133 = (f32[64,64,128]{2,1,0:T(8,128)}, f32[64,128]{1,0:T(8,128)}, f32[512,128]{1,0:T(8,128)S(1)}) custom-call(f32[64,64,128]{2,1,0:T(8,128)S(1)} %copy-done.1, f32[64,64,128]{2,1,0:T(8,128)S(1)} %get-tuple-element.17.x_ref, f32[64,128]{1,0:T(8,128)S(1)} %collective-permute-done.12.n_ref, f32[64,128]{1,0:T(8,128)S(1)} %collective-permute-done.13.s_ref, ...), custom_call_target="tpu_custom_call" | custom-call | tf_op jit(solution)/shard_map/pallas_call | solution.py:230
  166.3 18.3 %all_to_all.46 = f32[32,16,128]{2,1,0:T(8,128)S(1)} all-to-all(f32[32,16,128]{2,1,0:T(8,128)S(1)} %bitcast.77), channel_id=1, replica_groups=mesh['lat'=4,'lon'=8] {'lat','lon'}, dimensions={0} | all-to-all | bytes 524288 | tf_op jit(solution)/shard_map/all_to_all | solution.py:255
  184.7 12.8 %all_to_all.47 = f32[32,16,128]{2,1,0:T(8,128)S(1)} all-to-all(f32[32,16,128]{2,1,0:T(8,128)S(1)} %broadcast_in_dim.13), channel_id=1, replica_groups=mesh['lat'=4,'lon'=8] {'lat','lon'}, dimensions={0} | all-to-all | bytes 524288 | tf_op jit(solution)/shard_map/all_to_all | solution.py:255
  197.6 0.8 copy.46
  198.4 0.8 copy.45
  (68 shorter events, 1.5 us)
Async XLA Ops:
  0.6 89.2 %copy-start = (f32[128,64]{0,1:T(8,128)S(1)}, f32[128,64]{0,1:T(8,128)}, u32[]{:S(2)}) copy-start(f32[128,64]{0,1:T(8,128)} %param.14) | copy-start | bytes 98308
  5.7 11.6 %copy-start.1 = (f32[64,64,128]{2,1,0:T(8,128)S(1)}, f32[64,64,128]{2,1,0:T(8,128)}, u32[]{:S(2)}) copy-start(f32[64,64,128]{2,1,0:T(8,128)} %v_ref.1) | copy-start | bytes 6291460
  5.7 15.9 %copy-start.8 = (s32[256,1]{0,1:T(1,128)S(1)}, s32[256,1]{0,1:T(1,128)}, u32[]{:S(2)}) copy-start(s32[256,1]{0,1:T(1,128)} %param.17) | copy-start | bytes 3076
  5.7 16.9 %copy-start.9 = (f32[5,64]{1,0:T(8,128)S(1)}, f32[5,64]{1,0:T(8,128)}, u32[]{:S(2)}) copy-start(f32[5,64]{1,0:T(8,128)} %param.11) | copy-start | bytes 3844
  5.7 17.0 %copy-start.6 = (bf16[64,512]{1,0:T(8,128)(2,1)S(1)}, bf16[64,512]{1,0:T(8,128)(2,1)}, u32[]{:S(2)}) copy-start(bf16[64,512]{1,0:T(8,128)(2,1)} %wi_ref.3) | copy-start | bytes 196612
  5.7 18.1 %copy-start.7 = (bf16[512,64]{0,1:T(8,128)(2,1)S(1)}, bf16[512,64]{0,1:T(8,128)(2,1)}, u32[]{:S(2)}) copy-start(bf16[512,64]{0,1:T(8,128)(2,1)} %param.13) | copy-start | bytes 196612
  11.1 31.9 %copy-start.10 = (s32[256,4]{0,1:T(4,128)S(1)}, s32[256,4]{0,1:T(4,128)}, u32[]{:S(2)}) copy-start(s32[256,4]{0,1:T(4,128)} %param.18) | copy-start | bytes 12292
  11.2 11.6 %collective-permute-start.3 = (f32[64,128]{1,0:T(8,128)S(1)}, f32[64,128]{1,0:T(8,128)S(1)}, u32[]{:S(2)}, u32[]{:S(2)}) collective-permute-start(f32[64,128]{1,0:T(8,128)S(1)} %pad_maximum_fusion), channel_id=1, source_target_pairs={{1,0},{2,1},{3,2},{4,3},{5,4},{6,5},{7,6},{0,7},{9,8},{10,9},{11,1... | collective-permute-start | bytes 98312 | tf_op jit(solution)/shard_map/ppermute | solution.py:250
  17.2 6.6 %collective-permute-start.2 = (f32[64,128]{1,0:T(8,128)S(1)}, f32[64,128]{1,0:T(8,128)S(1)}, u32[]{:S(2)}, u32[]{:S(2)}) collective-permute-start(f32[64,128]{1,0:T(8,128)S(1)} %pad_maximum_fusion), channel_id=1, source_target_pairs={{0,1},{1,2},{2,3},{3,4},{4,5},{5,6},{6,7},{7,0},{8,9},{9,10},{10,1... | collective-permute-start | bytes 98312 | tf_op jit(solution)/shard_map/ppermute | solution.py:249
  17.2 5.5 %collective-permute-start.1 = (f32[64,128]{1,0:T(8,128)S(1)}, f32[64,128]{1,0:T(8,128)S(1)}, u32[]{:S(2)}, u32[]{:S(2)}) collective-permute-start(f32[64,128]{1,0:T(8,128)S(1)} %get-tuple-element.38), channel_id=1, source_target_pairs={{8,0},{16,8},{24,16},{9,1},{17,9},{25,17},{10,2},{18,10},{26,18},{... | collective-permute-start | bytes 98312 | tf_op jit(solution)/shard_map/ppermute | solution.py:248
  18.5 4.2 %collective-permute-start = (f32[64,128]{1,0:T(8,128)S(1)}, f32[64,128]{1,0:T(8,128)S(1)}, u32[]{:S(2)}, u32[]{:S(2)}) collective-permute-start(f32[64,128]{1,0:T(8,128)S(1)} %get-tuple-element.39), channel_id=1, source_target_pairs={{0,8},{8,16},{16,24},{1,9},{9,17},{17,25},{2,10},{10,18},{18,26},{... | collective-permute-start | bytes 98312 | tf_op jit(solution)/shard_map/ppermute | solution.py:247
  33.2 26.2 %collective-permute-start.7 = (f32[64,128]{1,0:T(8,128)S(1)}, f32[64,128]{1,0:T(8,128)S(1)}, u32[]{:S(2)}, u32[]{:S(2)}) collective-permute-start(f32[64,128]{1,0:T(8,128)S(1)} %get-tuple-element.14), channel_id=1, source_target_pairs={{1,0},{2,1},{3,2},{4,3},{5,4},{6,5},{7,6},{0,7},{9,8},{10,9},{11,1... | collective-permute-start | bytes 98312 | tf_op jit(solution)/shard_map/ppermute | solution.py:250
  37.0 22.4 %collective-permute-start.6 = (f32[64,128]{1,0:T(8,128)S(1)}, f32[64,128]{1,0:T(8,128)S(1)}, u32[]{:S(2)}, u32[]{:S(2)}) collective-permute-start(f32[64,128]{1,0:T(8,128)S(1)} %get-tuple-element.14), channel_id=1, source_target_pairs={{0,1},{1,2},{2,3},{3,4},{4,5},{5,6},{6,7},{7,0},{8,9},{9,10},{10,1... | collective-permute-start | bytes 98312 | tf_op jit(solution)/shard_map/ppermute | solution.py:249
  37.0 1.3 copy-start.2
  38.3 21.1 %collective-permute-start.5 = (f32[64,128]{1,0:T(8,128)S(1)}, f32[64,128]{1,0:T(8,128)S(1)}, u32[]{:S(2)}, u32[]{:S(2)}) collective-permute-start(f32[64,128]{1,0:T(8,128)S(1)} %get-tuple-element.34), channel_id=1, source_target_pairs={{8,0},{16,8},{24,16},{9,1},{17,9},{25,17},{10,2},{18,10},{26,18},{... | collective-permute-start | bytes 98312 | tf_op jit(solution)/shard_map/ppermute | solution.py:248
  39.6 19.8 %collective-permute-start.4 = (f32[64,128]{1,0:T(8,128)S(1)}, f32[64,128]{1,0:T(8,128)S(1)}, u32[]{:S(2)}, u32[]{:S(2)}) collective-permute-start(f32[64,128]{1,0:T(8,128)S(1)} %get-tuple-element.35), channel_id=1, source_target_pairs={{0,8},{8,16},{16,24},{1,9},{9,17},{17,25},{2,10},{10,18},{18,26},{... | collective-permute-start | bytes 98312 | tf_op jit(solution)/shard_map/ppermute | solution.py:247
  59.2 30.6 %copy-start.11 = (f32[256,128]{1,0:T(8,128)S(1)}, f32[256,128]{1,0:T(8,128)}, u32[]{:S(2)}) copy-start(f32[256,128]{1,0:T(8,128)} %param.16) | copy-start | bytes 393220
  59.2 30.6 %copy-start.12 = (s32[256]{0:T(256)S(1)}, s32[256]{0:T(256)}, u32[]{:S(2)}) copy-start(s32[256]{0:T(256)} %param.19) | copy-start | bytes 3076
  59.3 30.6 %copy-start.13 = (f32[128]{0:T(128)S(1)}, f32[128]{0:T(128)}, u32[]{:S(2)}) copy-start(f32[128]{0:T(128)} %param.15) | copy-start | bytes 1540
  59.4 1.6 copy-start.3
  77.1 10.4 %all-to-all-start.1 = ((f32[32,1,1024]{2,1,0:T(1,128)}), f32[32,1,1024]{2,1,0:T(1,128)S(1)}, u32[]{:S(2)}, u32[]{:S(2)}) async-start(f32[32,1,1024]{2,1,0:T(1,128)} %reshape.82), calls=%async_computation.1 | async-start | bytes 262144 | tf_op jit(solution)/shard_map/all_to_all | solution.py:255
  90.1 51.0 %copy-start.14 = (f32[256,128]{1,0:T(8,128)}, f32[256,128]{1,0:T(8,128)S(1)}, u32[]{:S(2)}) copy-start(f32[256,128]{1,0:T(8,128)S(1)} %fusion.1) | copy-start | bytes 393220
  115.2 2.1 %copy-start.5 = (f32[64,64,128]{2,1,0:T(8,128)}, f32[64,64,128]{2,1,0:T(8,128)S(1)}, u32[]{:S(2)}) copy-start(f32[64,64,128]{2,1,0:T(8,128)S(1)} %get-tuple-element.15.x_ref) | copy-start | bytes 6291460
  115.2 6.6 %collective-permute-start.11 = (f32[64,128]{1,0:T(8,128)S(1)}, f32[64,128]{1,0:T(8,128)S(1)}, u32[]{:S(2)}, u32[]{:S(2)}) collective-permute-start(f32[64,128]{1,0:T(8,128)S(1)} %get-tuple-element.16), channel_id=1, source_target_pairs={{1,0},{2,1},{3,2},{4,3},{5,4},{6,5},{7,6},{0,7},{9,8},{10,9},{11,1... | collective-permute-start | bytes 98312 | tf_op jit(solution)/shard_map/ppermute | solution.py:250
  117.2 6.6 %collective-permute-start.10 = (f32[64,128]{1,0:T(8,128)S(1)}, f32[64,128]{1,0:T(8,128)S(1)}, u32[]{:S(2)}, u32[]{:S(2)}) collective-permute-start(f32[64,128]{1,0:T(8,128)S(1)} %get-tuple-element.16), channel_id=1, source_target_pairs={{0,1},{1,2},{2,3},{3,4},{4,5},{5,6},{6,7},{7,0},{8,9},{9,10},{10,1... | collective-permute-start | bytes 98312 | tf_op jit(solution)/shard_map/ppermute | solution.py:249
  117.3 6.5 %collective-permute-start.9 = (f32[64,128]{1,0:T(8,128)S(1)}, f32[64,128]{1,0:T(8,128)S(1)}, u32[]{:S(2)}, u32[]{:S(2)}) collective-permute-start(f32[64,128]{1,0:T(8,128)S(1)} %get-tuple-element.32), channel_id=1, source_target_pairs={{8,0},{16,8},{24,16},{9,1},{17,9},{25,17},{10,2},{18,10},{26,18},{... | collective-permute-start | bytes 98312 | tf_op jit(solution)/shard_map/ppermute | solution.py:248
  118.6 5.2 %collective-permute-start.8 = (f32[64,128]{1,0:T(8,128)S(1)}, f32[64,128]{1,0:T(8,128)S(1)}, u32[]{:S(2)}, u32[]{:S(2)}) collective-permute-start(f32[64,128]{1,0:T(8,128)S(1)} %get-tuple-element.33), channel_id=1, source_target_pairs={{0,8},{8,16},{16,24},{1,9},{9,17},{17,25},{2,10},{10,18},{18,26},{... | collective-permute-start | bytes 98312 | tf_op jit(solution)/shard_map/ppermute | solution.py:247
  123.8 1.6 copy-start.4
  141.1 7.7 %collective-permute-start.15 = (f32[64,128]{1,0:T(8,128)S(1)}, f32[64,128]{1,0:T(8,128)S(1)}, u32[]{:S(2)}, u32[]{:S(2)}) collective-permute-start(f32[64,128]{1,0:T(8,128)S(1)} %get-tuple-element.18), channel_id=1, source_target_pairs={{1,0},{2,1},{3,2},{4,3},{5,4},{6,5},{7,6},{0,7},{9,8},{10,9},{11,1... | collective-permute-start | bytes 98312 | tf_op jit(solution)/shard_map/ppermute | solution.py:250
  144.4 6.6 %collective-permute-start.14 = (f32[64,128]{1,0:T(8,128)S(1)}, f32[64,128]{1,0:T(8,128)S(1)}, u32[]{:S(2)}, u32[]{:S(2)}) collective-permute-start(f32[64,128]{1,0:T(8,128)S(1)} %get-tuple-element.18), channel_id=1, source_target_pairs={{0,1},{1,2},{2,3},{3,4},{4,5},{5,6},{6,7},{7,0},{8,9},{9,10},{10,1... | collective-permute-start | bytes 98312 | tf_op jit(solution)/shard_map/ppermute | solution.py:249
  144.5 6.6 %collective-permute-start.13 = (f32[64,128]{1,0:T(8,128)S(1)}, f32[64,128]{1,0:T(8,128)S(1)}, u32[]{:S(2)}, u32[]{:S(2)}) collective-permute-start(f32[64,128]{1,0:T(8,128)S(1)} %get-tuple-element.30), channel_id=1, source_target_pairs={{8,0},{16,8},{24,16},{9,1},{17,9},{25,17},{10,2},{18,10},{26,18},{... | collective-permute-start | bytes 98312 | tf_op jit(solution)/shard_map/ppermute | solution.py:248
  145.8 5.3 %collective-permute-start.12 = (f32[64,128]{1,0:T(8,128)S(1)}, f32[64,128]{1,0:T(8,128)S(1)}, u32[]{:S(2)}, u32[]{:S(2)}) collective-permute-start(f32[64,128]{1,0:T(8,128)S(1)} %get-tuple-element.31), channel_id=1, source_target_pairs={{0,8},{8,16},{16,24},{1,9},{9,17},{17,25},{2,10},{10,18},{18,26},{... | collective-permute-start | bytes 98312 | tf_op jit(solution)/shard_map/ppermute | solution.py:247

commit v2 on v1

--- a/solution.py
+++ b/solution.py
@@ -140,14 +140,17 @@
         return carry
 
     lax.fori_loop(0, count // GROUP, step, 0)
-    o_ref[...] = jnp.transpose(acc[...] * TENTH)
+    blocks = jnp.transpose(acc[...] * TENTH).reshape(slots // CAP, CAP, feat)
+    o_ref[...] = jnp.concatenate([blocks[:, : CAP // 2], blocks[:, CAP // 2 :]], axis=2)
 
 
 def spread_kernel(pulled_ref, cell_ref, o_ref, edge_ref, parts):
     count, feat, width = o_ref.shape
     slots = cell_ref.shape[0]
     edge_ref[...] = jnp.zeros_like(edge_ref)
-    parts[...] = two_parts(jnp.transpose(pulled_ref[...]) * TENTH)
+    blocks = pulled_ref[...]
+    pulled = jnp.concatenate([blocks[:, :, :feat], blocks[:, :, feat:]], axis=1)
+    parts[...] = two_parts(jnp.transpose(pulled.reshape(slots, feat)) * TENTH)
     block = min(slots, 512)
 
     def step(b, carry):
@@ -237,22 +240,138 @@
     )(*args)
 
 
-def halos(field, edges):
-    lat, lon = lax.axis_size("lat"), lax.axis_size("lon")
-    south = [(i, i + 1) for i in range(lat - 1)]
-    north = [(i + 1, i) for i in range(lat - 1)]
-    east = [(i, (i + 1) % lon) for i in range(lon)]
-    west = [((i + 1) % lon, i) for i in range(lon)]
-    return (
-        lax.ppermute(field[-1], "lat", south),
-        lax.ppermute(field[0], "lat", north),
-        lax.ppermute(edges, "lon", east),
-        lax.ppermute(edges, "lon", west),
-    )
-
-
-def swap(blocks):
-    return lax.all_to_all(blocks, ("lat", "lon"), split_axis=0, concat_axis=0, tiled=True)
+def place(index):
+    lon = lax.axis_size("lon")
+    return {"lat": index // lon, "lon": lax.rem(index, lon)}
+
+
+def remote(src, dst, send, recv, to):
+    return pltpu.make_async_remote_copy(
+        src_ref=src,
+        dst_ref=dst,
+        send_sem=send,
+        recv_sem=recv,
+        device_id=to,
+        device_id_type=pl.DeviceIdType.MESH,
+    )
+
+
+def signal(sem, to):
+    pl.semaphore_signal(sem, inc=1, device_id=to, device_id_type=pl.DeviceIdType.MESH)
+
+
+def exchange_kernel(mode, halo, *refs):
+    refs = list(refs)
+    take = lambda k: [refs.pop(0) for _ in range(k)]
+    field, edges = take(2) if halo else (None, None)
+    (blocks,) = take(1) if mode else (None,)
+    halo_out = take(4) if halo else ()
+    (blocks_out,) = take(1) if mode else (None,)
+    halo_send, halo_recv = take(2) if halo else (None, None)
+    send, recv, own_sem = take(3) if mode else (None, None, None)
+
+    lat, lon = lax.axis_index("lat"), lax.axis_index("lon")
+    lats, lons = lax.axis_size("lat"), lax.axis_size("lon")
+    devices = lats * lons
+    me = lat * lons + lon
+    south, north = {"lat": lax.rem(lat + 1, lats)}, {"lat": lax.rem(lat + lats - 1, lats)}
+    east, west = {"lon": lax.rem(lon + 1, lons)}, {"lon": lax.rem(lon + lons - 1, lons)}
+
+    barrier = pltpu.get_barrier_semaphore()
+    if mode:
+
+        def greet(k, carry):
+            signal(barrier, place(lax.rem(me + k, devices)))
+            return carry
+
+        lax.fori_loop(1, devices, greet, 0)
+        pl.semaphore_wait(barrier, devices - 1)
+    else:
+        for to in (south, north, east, west):
+            signal(barrier, to)
+        pl.semaphore_wait(barrier, 4)
+
+    halo_copies = []
+    if halo:
+        count = field.shape[0]
+        sources = (field.at[count - 1], field.at[0], edges, edges)
+        for k, to in enumerate((south, north, east, west)):
+            halo_copies.append(
+                remote(sources[k], halo_out[k], halo_send.at[k], halo_recv.at[k], to)
+            )
+            halo_copies[-1].start()
+    if mode:
+
+        def copy_to(k):
+            peer = lax.rem(me + k, devices)
+            source = blocks.at[peer] if mode == "swap" else blocks
+            return remote(source, blocks_out.at[me], send.at[k], recv.at[k], place(peer))
+
+        def start(k, carry):
+            copy_to(k).start()
+            return carry
+
+        def finish(k, carry):
+            copy_to(k).wait()
+            return carry
+
+        lax.fori_loop(1, devices, start, 0)
+        own = pltpu.make_async_copy(
+            blocks.at[me] if mode == "swap" else blocks, blocks_out.at[me], own_sem.at[0]
+        )
+        own.start()
+        own.wait()
+        lax.fori_loop(1, devices, finish, 0)
+    for copy in halo_copies:
+        copy.wait()
+    if halo:
+
+        @pl.when(lat == 0)
+        def _():
+            halo_out[0][...] = jnp.zeros_like(halo_out[0])
+
+        @pl.when(lat == lats - 1)
+        def _():
+            halo_out[1][...] = jnp.zeros_like(halo_out[1])
+
+
+def exchange(number, mode=None, blocks=None, field=None, edges=None):
+    devices = lax.axis_size("lat") * lax.axis_size("lon")
+    halo = field is not None
+    vmem, dma = pl.BlockSpec(memory_space=pltpu.VMEM), pltpu.SemaphoreType.DMA
+    args, specs, outs, scratch = [], [], [], []
+    if halo:
+        args += [field, edges]
+        specs += [pl.BlockSpec(memory_space=pl.ANY), vmem]
+        outs += [jax.ShapeDtypeStruct(edges.shape, edges.dtype)] * 4
+        scratch += [dma((4,)), dma((4,))]
+    if mode:
+        block = blocks.shape[1:] if mode == "swap" else blocks.shape
+        args.append(blocks)
+        specs.append(vmem)
+        outs.append(jax.ShapeDtypeStruct((devices,) + block, blocks.dtype))
+        scratch += [dma((devices,)), dma((devices,)), dma((1,))]
+    return pl.pallas_call(
+        functools.partial(exchange_kernel, mode, halo),
+        out_shape=outs,
+        in_specs=specs,
+        out_specs=[vmem] * len(outs),
+        scratch_shapes=scratch,
+        compiler_params=pltpu.CompilerParams(
+            collective_id=number, has_side_effects=True, vmem_limit_bytes=16 * 1024 * 1024
+        ),
+    )(*args)
+
+
+def edge_kernel(x_ref, edge_ref):
+    count = x_ref.shape[0]
+    edge_ref[...] = jnp.zeros_like(edge_ref)
+
+    def step(i, carry):
+        keep_edges(edge_ref, x_ref[i], i, count)
+        return carry
+
+    lax.fori_loop(0, count, step, 0, unroll=4)
 
 
 def f32(*shape):
@@ -280,33 +399,44 @@
     rank = jnp.sum(running * onehot, axis=1) - 1
     slot = tile_owner * CAP + rank
     send_stencil = jnp.zeros((slots, 4), jnp.int32).at[slot].set(stencil)
-    cell_recv = swap(send_stencil)
 
     coef = coefficients.T
     w_in_t, w_out_t = w_in.T, w_out.T
-    start_edges = jnp.concatenate([start_state[:, :, 0].T, start_state[:, :, -1].T], axis=1)
+    start_edges = call(edge_kernel, edge_shape, [], start_state)
     state_one, edges_one = call(
         forward_kernel,
         (tile, edge_shape),
         [rows_scratch],
         start_state,
-        *halos(start_state, start_edges),
+        *exchange(0, field=start_state, edges=start_edges),
         coef,
         w_in_t,
         w_out_t,
     )
+    *halo_one, cell_recv = exchange(
+        1,
+        "swap",
+        send_stencil.reshape(devices, 1, CAP * 4),
+        field=state_one,
+        edges=edges_one,
+    )
+    cell_recv = cell_recv.reshape(slots, 4)
     slot_interp = call(
         forward_interp_kernel,
-        f32(slots, feat),
+        f32(devices, CAP // 2, 2 * feat),
         [rows_scratch, pltpu.VMEM((feat, slots), jnp.float32)],
         state_one,
-        *halos(state_one, edges_one),
+        *halo_one,
         coef,
         w_in_t,
         w_out_t,
         cell_recv.T,
     )
-    row_interp = swap(slot_interp)[slot]
+    half = (rank >= CAP // 2)[:, None]
+    packed = tile_owner * (CAP // 2) + rank % (CAP // 2)
+    (interp,) = exchange(2, "swap", slot_interp)
+    both = interp.reshape(slots // 2, 2 * feat)[packed]
+    row_interp = jnp.where(half, both[:, feat:], both[:, :feat])
     evolved = jnp.dot(
         row_interp, jacobian.T, precision=lax.Precision.HIGHEST, preferred_element_type=jnp.float32
     )
@@ -318,7 +448,13 @@
         precision=lax.Precision.HIGHEST,
         preferred_element_type=jnp.float32,
     )
-    recv_pulled = swap(jnp.zeros((slots, feat), jnp.float32).at[slot].set(row_pulled))
+    row_pair = jnp.concatenate(
+        [jnp.where(half, 0.0, row_pulled), jnp.where(half, row_pulled, 0.0)], axis=1
+    )
+    send_pulled = jnp.zeros((slots // 2, 2 * feat), jnp.float32).at[packed].add(row_pair)
+    (recv_pulled,) = exchange(
+        3, "swap", send_pulled.reshape(devices, CAP // 2, 2 * feat)
+    )
     adjoint_two, edges_two = call(
         spread_kernel,
         (tile, edge_shape),
@@ -327,27 +463,26 @@
         cell_recv,
     )
 
-    def backward(state, cotangent, edges):
+    def backward(number, state, cotangent, edges):
         return call(
             backward_kernel,
             (tile, edge_shape, f32(hid, 2 * feat)),
             [rows_scratch] + [pltpu.VMEM((hid, feat), jnp.float32)] * 2,
             state,
             cotangent,
-            *halos(cotangent, edges),
+            *exchange(number, field=cotangent, edges=edges),
             coef,
             w_in_t,
             w_in,
             w_out,
         )
 
-    adjoint_one, edges_adj, grads_one = backward(state_one, adjoint_two, edges_two)
-    grad_state, _, grads_zero = backward(start_state, adjoint_one, edges_adj)
+    adjoint_one, edges_adj, grads_one = backward(4, state_one, adjoint_two, edges_two)
+    grad_state, _, grads_zero = backward(5, start_state, adjoint_one, edges_adj)
     grads = (grads_one + grads_zero).reshape(devices, hid // devices, 2 * feat)
-    part = jnp.sum(swap(grads), axis=0)
+    part = jnp.sum(exchange(6, "swap", grads)[0], axis=0)
     scale = 1.0 / math.sqrt(tlat * lat_count * tlon * lon_count)
-    part = part * scale
-    total = swap(jnp.broadcast_to(part[None], grads.shape)).reshape(hid, 2 * feat)
+    total = exchange(7, "spread", part * scale)[0].reshape(hid, 2 * feat)
     return (grad_state, departures, total[:, :feat].T, total[:, feat:])
 
 

time: 200 us -> 162 us (0.81)
  Pallas kernels: 68 us -> 145 us
  blocking collectives: 55.3 us -> 0 us
  starting transfers between devices: 35.4 us -> 0 us
  waiting for transfers between devices: 13.1 us -> 0 us
  local copies, waits for them, and re-layouts: 22.9 us -> 10.5 us
  other arithmetic: 2.79 us -> 5.09 us
    pallas_call x0 -> x8, Pallas kernels: none -> 74.5 us  [exchange(): pl.pallas_call(functools.partial(exchange_kernel, mode, halo), out_shape=...]
    all_to_all x4 -> x0, blocking collectives: 55.3 us -> none  [swap(): lax.all_to_all(blocks, ('lat', 'lon'), split_axis=0, concat_axis=0, tiled...]
    ppermute x16 -> x0, starting transfers between devices: 32.9 us -> none  [the longest x4 15.1 us: halos(): lax.ppermute(edges, 'lon', west)]
    all_to_all x1 -> x0, waiting for transfers between devices: 7.79 us -> none  [swap(): lax.all_to_all(blocks, ('lat', 'lon'), split_axis=0, concat_axis=0, tiled...]
    unnamed x42 -> x34, local copies, waits for them, and re-layouts: 13.2 us -> 7.27 us
    ppermute x16 -> x0, waiting for transfers between devices: 5.35 us -> none  [the longest x4 5.32 us: halos(): lax.ppermute(edges, 'lon', east)]
    slice x2 -> x1, local copies, waits for them, and re-layouts: 5.2 us -> 0.18 us  [the longest x1 5.01 us: on_device(): start_state[:, :, 0]]
    all_to_all x1 -> x0, starting transfers between devices: 2.58 us -> none  [swap(): lax.all_to_all(blocks, ('lat', 'lon'), split_axis=0, concat_axis=0, tiled...]
  transfers between devices with their start and end apart: 17 -> 0, of which waited for: 4 -> 0; matrix products, arithmetic and copies ran while one was open for 2% -> 0% of each run, Pallas kernels for 0% -> 0%
where the time goes in v2:
time: 162 us
  Pallas kernels  145 us (90%)
  local copies, waits for them, and re-layouts  10.5 us (6%)
  other arithmetic  5.09 us (3%)
    pallas_call x8, Pallas kernels, exchange(): pl.pallas_call(functools.partial(exchange_kernel, mode, halo), out_shape=...  74.5 us
    pallas_call x6, Pallas kernels, call(): pl.pallas_call(kernel, out_shape=outs, in_specs=[pl.BlockSpec(memory_spac...  70.3 us
    unnamed x34, local copies, waits for them, and re-layouts  7.27 us

profile of v2, /device:TPU:0, one launch (start us, length us, event | category | flops | bytes accessed | tf_op | source)
XLA Modules:
  0.0 162.0 jit_solution(12375989339419144688)
XLA Ops:
  0.6 0.0 copy-start
  0.6 0.8 copy.23
  1.4 0.7 fusion.17
  2.1 0.6 reduce-window.6
  2.7 0.2 slice_reduce_fusion
  2.9 0.8 fusion.16
  3.7 0.7 compare_select_fusion
  4.4 0.0 copy-start.1
  4.4 1.6 copy-done.1
  6.0 2.2 %shard_map.129.refs_1_ = f32[64,128]{1,0:T(8,128)S(1)} custom-call(f32[64,64,128]{2,1,0:T(8,128)S(1)} %copy-done.1), custom_call_target="tpu_custom_call" | custom-call | tf_op jit(solution)/shard_map/pallas_call | solution.py:233
  8.2 0.0 copy-start.2
  8.2 9.3 %shard_map.130 = (f32[64,128]{1,0:T(8,128)S(1)}, f32[64,128]{1,0:T(8,128)S(1)}, f32[64,128]{1,0:T(8,128)S(1)}, f32[64,128]{1,0:T(8,128)S(1)}) custom-call(f32[64,64,128]{2,1,0:T(8,128)S(1)} %copy-done.1, f32[64,128]{1,0:T(8,128)S(1)} %shard_map.129.refs_1_), custom_call_target="tpu_custom_call" | custom-call | tf_op jit(solution)/shard_map/pallas_call | solution.py:354
  17.5 0.1 copy.31.wo_ref
  17.7 0.1 copy.26
  17.8 1.2 scatter_custom_fusion
  19.0 0.1 reshape.94
  19.2 0.1 copy.24
  19.3 9.4 %shard_map.131 = (f32[64,64,128]{2,1,0:T(8,128)S(1)}, f32[64,128]{1,0:T(8,128)S(1)}) custom-call(f32[64,64,128]{2,1,0:T(8,128)S(1)} %copy-done.2, f32[64,128]{1,0:T(8,128)S(1)} %get-tuple-element.30.n_ref, f32[64,128]{1,0:T(8,128)S(1)} %get-tuple-element.31.s_ref, f32[64,128]{1,0:T(8,128)S(1)} %get-tuple-element.32.l_ref, ...), custom_call_target="tpu_custom_call" | custom-call | tf_op jit(solution)/shard_map/pallas_call | solution.py:233
  28.7 9.0 %shard_map.132 = (f32[64,128]{1,0:T(8,128)S(1)}, f32[64,128]{1,0:T(8,128)S(1)}, f32[64,128]{1,0:T(8,128)S(1)}, f32[64,128]{1,0:T(8,128)S(1)}, s32[32,1,64]{2,1,0:T(1,128)S(1)}) custom-call(f32[64,64,128]{2,1,0:T(8,128)S(1)} %get-tuple-element.34.refs_0_.x_ref.v_ref, f32[64,128]{1,0:T(8,128)S(1)} %get-tuple-element.35.refs_1_, s32[32,1,64]{2,1,0:T(1,128)S(1)} %bitcast.47), custom_call_target="tpu_custom_call" | custom-call | tf_op jit(solution)/shard_map/pallas_call | solution.py:354
  37.7 0.0 copy-start.3
  37.7 1.3 copy-done.3
  39.0 0.5 broadcast.119
  39.5 0.7 reduce.5
  40.2 0.2 reshape.95.cell_ref
  40.4 0.0 copy-start.10
  40.4 0.0 copy-start.11
  40.4 0.0 copy-start.12
  40.4 0.1 copy.28
  40.5 1.6 copy-done.4
  42.1 15.4 %shard_map.133.refs_0_ = f32[32,8,128]{2,1,0:T(8,128)S(1)} custom-call(f32[64,64,128]{2,1,0:T(8,128)S(1)} %copy-done.4, f32[64,128]{1,0:T(8,128)S(1)} %get-tuple-element.36.n_ref, f32[64,128]{1,0:T(8,128)S(1)} %get-tuple-element.37.s_ref, f32[64,128]{1,0:T(8,128)S(1)} %get-tuple-element.38.l_ref, f32[64,128]{1,0:T(8,128)S(1)} %get-tuple-element.39.r_ref, ...), custom_call_target="tpu_custom_call" | custom-call | tf_op jit(solution)/shard_map/pallas_call | solution.py:233
  57.5 9.4 %shard_map.134 = f32[32,8,128]{2,1,0:T(8,128)S(1)} custom-call(f32[32,8,128]{2,1,0:T(8,128)S(1)} %shard_map.133.refs_0_), custom_call_target="tpu_custom_call" | custom-call | tf_op jit(solution)/shard_map/pallas_call | solution.py:354
  66.9 0.7 gather_fusion
  67.7 0.3 fusion.1
  68.0 0.0 copy-start.13
  68.1 0.3 broadcast_select_fusion.1
  68.3 1.6 scatter_custom_fusion.1
  69.9 0.0 copy-start.5
  69.9 9.4 %shard_map.135.pulled_ref = f32[32,8,128]{2,1,0:T(8,128)S(1)} custom-call(f32[32,8,128]{2,1,0:T(8,128)S(1)} %bitcast.46), custom_call_target="tpu_custom_call" | custom-call | tf_op jit(solution)/shard_map/pallas_call | solution.py:354
  79.3 12.5 %shard_map.136 = (f32[64,64,128]{2,1,0:T(8,128)S(1)}, f32[64,128]{1,0:T(8,128)S(1)}) custom-call(f32[32,8,128]{2,1,0:T(8,128)S(1)} %shard_map.135.pulled_ref, s32[512,4]{1,0:T(8,128)S(1)} %reshape.95.cell_ref), custom_call_target="tpu_custom_call" | custom-call | tf_op jit(solution)/shard_map/pallas_call | solution.py:233
  91.8 6.7 %shard_map.137 = (f32[64,128]{1,0:T(8,128)S(1)}, f32[64,128]{1,0:T(8,128)S(1)}, f32[64,128]{1,0:T(8,128)S(1)}, f32[64,128]{1,0:T(8,128)S(1)}) custom-call(f32[64,64,128]{2,1,0:T(8,128)S(1)} %get-tuple-element.41.refs_0_.x_ref, f32[64,128]{1,0:T(8,128)S(1)} %get-tuple-element.42.refs_1_), custom_call_target="tpu_custom_call" | custom-call | tf_op jit(solution)/shard_map/pallas_call | solution.py:354
  98.6 15.7 %shard_map.138 = (f32[64,64,128]{2,1,0:T(8,128)S(1)}, f32[64,128]{1,0:T(8,128)S(1)}, f32[512,128]{1,0:T(8,128)S(1)}) custom-call(f32[64,64,128]{2,1,0:T(8,128)S(1)} %copy-done.5, f32[64,64,128]{2,1,0:T(8,128)} %copy-done.6, f32[64,128]{1,0:T(8,128)S(1)} %get-tuple-element.43.n_ref, f32[64,128]{1,0:T(8,128)S(1)} %get-tuple-element.44.s_ref, ...), custom_call_target="tpu_custom_call" | custom-call | tf_op jit(solution)/shard_map/pallas_call | solution.py:233
  114.3 6.7 %shard_map.139 = (f32[64,128]{1,0:T(8,128)S(1)}, f32[64,128]{1,0:T(8,128)S(1)}, f32[64,128]{1,0:T(8,128)S(1)}, f32[64,128]{1,0:T(8,128)S(1)}) custom-call(f32[64,64,128]{2,1,0:T(8,128)S(1)} %get-tuple-element.47.refs_0_.x_ref, f32[64,128]{1,0:T(8,128)S(1)} %get-tuple-element.48.refs_1_), custom_call_target="tpu_custom_call" | custom-call | tf_op jit(solution)/shard_map/pallas_call | solution.py:354
  121.1 15.2 %shard_map.140 = (f32[64,64,128]{2,1,0:T(8,128)}, f32[64,128]{1,0:T(8,128)}, f32[512,128]{1,0:T(8,128)S(1)}) custom-call(f32[64,64,128]{2,1,0:T(8,128)S(1)} %copy-done.2, f32[64,64,128]{2,1,0:T(8,128)S(1)} %get-tuple-element.47.refs_0_.x_ref, f32[64,128]{1,0:T(8,128)S(1)} %get-tuple-element.49.n_ref, f32[64,128]{1,0:T(8,128)S(1)} %get-tuple-element.50.s_ref, ...), custom_call_target="tpu_custom_call" | custom-call | tf_op jit(solution)/shard_map/pallas_call | solution.py:233
  136.3 11.9 %shard_map.141 = f32[32,16,128]{2,1,0:T(8,128)S(1)} custom-call(f32[32,16,128]{2,1,0:T(8,128)S(1)} %bitcast.39), custom_call_target="tpu_custom_call" | custom-call | tf_op jit(solution)/shard_map/pallas_call | solution.py:354
  148.3 12.0 %shard_map.142 = f32[32,16,128]{2,1,0:T(8,128)S(1)} custom-call(f32[16,128]{1,0:T(8,128)S(1)} %broadcast_multiply_fusion.refs_0_), custom_call_target="tpu_custom_call" | custom-call | tf_op jit(solution)/shard_map/pallas_call | solution.py:354
  160.3 0.1 fusion.20
  160.4 0.8 copy.37
  161.2 0.8 copy.36
  (24 shorter events, 0.2 us)
Async XLA Ops:
  0.6 67.0 %copy-start = (f32[128,64]{0,1:T(8,128)S(1)}, f32[128,64]{0,1:T(8,128)}, u32[]{:S(2)}) copy-start(f32[128,64]{0,1:T(8,128)} %param.14) | copy-start | bytes 98308
  4.4 1.6 copy-start.1
  6.0 11.5 %copy-start.8 = (bf16[512,64]{0,1:T(8,128)(2,1)S(1)}, bf16[512,64]{0,1:T(8,128)(2,1)}, u32[]{:S(2)}) copy-start(bf16[512,64]{0,1:T(8,128)(2,1)} %param.13) | copy-start | bytes 196612
  6.0 11.6 %copy-start.9 = (s32[256,4]{0,1:T(4,128)S(1)}, s32[256,4]{0,1:T(4,128)}, u32[]{:S(2)}) copy-start(s32[256,4]{0,1:T(4,128)} %param.18) | copy-start | bytes 12292
  6.0 13.2 %copy-start.7 = (bf16[64,512]{1,0:T(8,128)(2,1)S(1)}, bf16[64,512]{1,0:T(8,128)(2,1)}, u32[]{:S(2)}) copy-start(bf16[64,512]{1,0:T(8,128)(2,1)} %wi_ref.3) | copy-start | bytes 196612
  8.2 11.1 %copy-start.2 = (f32[64,64,128]{2,1,0:T(8,128)S(1)}, f32[64,64,128]{2,1,0:T(8,128)}, u32[]{:S(2)}) copy-start(f32[64,64,128]{2,1,0:T(8,128)} %v_ref.1) | copy-start | bytes 6291460
  37.7 1.3 copy-start.3
  40.4 27.3 %copy-start.10 = (f32[256,128]{1,0:T(8,128)S(1)}, f32[256,128]{1,0:T(8,128)}, u32[]{:S(2)}) copy-start(f32[256,128]{1,0:T(8,128)} %param.16) | copy-start | bytes 393220
  40.4 27.3 %copy-start.11 = (s32[256]{0:T(256)S(1)}, s32[256]{0:T(256)}, u32[]{:S(2)}) copy-start(s32[256]{0:T(256)} %param.19) | copy-start | bytes 3076
  40.4 27.3 %copy-start.12 = (f32[128]{0:T(128)S(1)}, f32[128]{0:T(128)}, u32[]{:S(2)}) copy-start(f32[128]{0:T(128)} %param.15) | copy-start | bytes 1540
  40.5 1.6 copy-start.4
  68.0 46.3 %copy-start.13 = (f32[256,128]{1,0:T(8,128)}, f32[256,128]{1,0:T(8,128)S(1)}, u32[]{:S(2)}) copy-start(f32[256,128]{1,0:T(8,128)S(1)} %fusion.1) | copy-start | bytes 393220
  69.9 28.7 %copy-start.5 = (f32[64,64,128]{2,1,0:T(8,128)S(1)}, f32[64,64,128]{2,1,0:T(8,128)}, u32[]{:S(2)}) copy-start(f32[64,64,128]{2,1,0:T(8,128)} %copy-done.3) | copy-start | bytes 6291460
  91.8 6.8 %copy-start.6 = (f32[64,64,128]{2,1,0:T(8,128)}, f32[64,64,128]{2,1,0:T(8,128)S(1)}, u32[]{:S(2)}) copy-start(f32[64,64,128]{2,1,0:T(8,128)S(1)} %get-tuple-element.41.refs_0_.x_ref) | copy-start | bytes 6291460

commit v3 on v2

--- a/solution.py
+++ b/solution.py
@@ -10,6 +10,7 @@
 
 CAP = 16
 GROUP = 4
+BACK_GROUP = 8
 VMEM_LIMIT = 48 * 1024 * 1024
 corner_tenths = (4, 3, 2, 1)
 TENTH = 0.1
@@ -76,6 +77,18 @@
     return jnp.concatenate([high, low], axis=0)
 
 
+def picks(local, cells):
+    slots = local.shape[1]
+    low = local.astype(jnp.int16)
+    cell = lax.broadcasted_iota(jnp.int16, (cells, slots), 0)
+    zero = jnp.zeros((cells, slots), jnp.bfloat16)
+    pick = zero
+    for k in range(4):
+        same = cell == jnp.broadcast_to(low[k : k + 1], (cells, slots))
+        pick = pick + jnp.where(same, jnp.full_like(zero, corner_tenths[k]), zero)
+    return pick
+
+
 def forward_group(rows, left, right, weights, wit_ref, wot_ref, base):
     width = rows.shape[2]
     inputs = jnp.concatenate([rows[base + g + 1] for g in range(GROUP)], axis=1).astype(
@@ -127,15 +140,7 @@
         )
         parts = two_parts(jnp.concatenate(out, axis=1))
         for s in range(0, slots, block):
-            cell = (
-                lax.broadcasted_iota(jnp.int32, (GROUP * width, block), 0) + base * width
-            )
-            pick = jnp.zeros((GROUP * width, block), jnp.float32)
-            for k in range(4):
-                pick = pick + jnp.where(
-                    cell == cell_ref[k : k + 1, s : s + block], float(corner_tenths[k]), 0.0
-                )
-            both = mm(parts, pick.astype(jnp.bfloat16))
+            both = mm(parts, picks(cell_ref[:, s : s + block] - base * width, GROUP * width))
             acc[:, s : s + block] += both[:feat] + both[feat:]
         return carry
 
@@ -146,7 +151,7 @@
 
 def spread_kernel(pulled_ref, cell_ref, o_ref, edge_ref, parts):
     count, feat, width = o_ref.shape
-    slots = cell_ref.shape[0]
+    slots = cell_ref.shape[1]
     edge_ref[...] = jnp.zeros_like(edge_ref)
     blocks = pulled_ref[...]
     pulled = jnp.concatenate([blocks[:, :, :feat], blocks[:, :, feat:]], axis=1)
@@ -157,15 +162,8 @@
         base = b * GROUP
         total = jnp.zeros((2 * feat, GROUP * width), jnp.float32)
         for s in range(0, slots, block):
-            cell = (
-                lax.broadcasted_iota(jnp.int32, (block, GROUP * width), 1) + base * width
-            )
-            pick = jnp.zeros((block, GROUP * width), jnp.float32)
-            for k in range(4):
-                pick = pick + jnp.where(
-                    cell == cell_ref[s : s + block, k : k + 1], float(corner_tenths[k]), 0.0
-                )
-            total = total + mm(parts[:, s : s + block], pick.astype(jnp.bfloat16))
+            pick = picks(cell_ref[:, s : s + block] - base * width, GROUP * width)
+            total = total + mm_nt(parts[:, s : s + block], pick)
         out = total[:feat] + total[feat:]
         for g in range(GROUP):
             row = out[:, g * width : (g + 1) * width]
@@ -201,12 +199,12 @@
     gout[...] = jnp.zeros_like(gout)
 
     def step(b, carry):
-        base = b * GROUP
+        base = b * BACK_GROUP
         weights = weights_of(c_ref, (0, 2, 1, 4, 3), width)
-        inputs = jnp.concatenate([v_ref[base + g] for g in range(GROUP)], axis=1).astype(
+        inputs = jnp.concatenate([v_ref[base + g] for g in range(BACK_GROUP)], axis=1).astype(
             jnp.bfloat16
         )
-        cot = jnp.concatenate([rows[base + g + 1] for g in range(GROUP)], axis=1).astype(
+        cot = jnp.concatenate([rows[base + g + 1] for g in range(BACK_GROUP)], axis=1).astype(
             jnp.bfloat16
         )
         tanh_pre = jnp.tanh(mm(wit_ref[...], inputs))
@@ -216,7 +214,7 @@
         back_pre = (back_hidden * (1.0 - tanh_pre * tanh_pre)).astype(jnp.bfloat16)
         gin[...] += mm_nt(back_pre, inputs)
         back = mm(wi_ref[...], back_pre)
-        for g in range(GROUP):
+        for g in range(BACK_GROUP):
             row = (
                 stencil_row(rows, l_ref[...], r_ref[...], weights, base + g)
                 + back[:, g * width : (g + 1) * width]
@@ -225,7 +223,7 @@
             keep_edges(edge_ref, row, base + g, count)
         return carry
 
-    lax.fori_loop(0, count // GROUP, step, 0)
+    lax.fori_loop(0, count // BACK_GROUP, step, 0)
     grad_ref[...] = jnp.concatenate([gin[...], gout[...]], axis=1)
 
 
@@ -382,6 +380,7 @@
     start_state, coefficients, w_in, w_out, jacobian, sigma, obs_values, owner, stencil, counts
 ):
     tlat, feat, tlon = start_state.shape
+    assert tlat * tlon <= 1 << 15
     hid = w_in.shape[1]
     lat_count = lax.axis_size("lat")
     lon_count = lax.axis_size("lon")
@@ -460,7 +459,7 @@
         (tile, edge_shape),
         [pltpu.VMEM((2 * feat, slots), jnp.bfloat16)],
         recv_pulled,
-        cell_recv,
+        cell_recv.T,
     )
 
     def backward(number, state, cotangent, edges):

time: 162 us -> 152 us (0.938)
  Pallas kernels: 145 us -> 135 us
    pallas_call x6, Pallas kernels: 70.3 us -> 60 us  [call(): pl.pallas_call(kernel, out_shape=outs, in_specs=[pl.BlockSpec(memory_spac...]
where the time goes in v3:
time: 152 us
  Pallas kernels  135 us (89%)
  local copies, waits for them, and re-layouts  10.5 us (7%)
  other arithmetic  5.09 us (3%)
    pallas_call x8, Pallas kernels, exchange(): pl.pallas_call(functools.partial(exchange_kernel, mode, halo), out_shape=...  74.6 us
    pallas_call x6, Pallas kernels, call(): pl.pallas_call(kernel, out_shape=outs, in_specs=[pl.BlockSpec(memory_spac...  60 us
    unnamed x34, local copies, waits for them, and re-layouts  7.27 us

profile of v3, /device:TPU:0, one launch (start us, length us, event | category | flops | bytes accessed | tf_op | source)
XLA Modules:
  0.0 151.8 jit_solution(4774188791711754870)
XLA Ops:
  0.6 0.0 copy-start
  0.6 0.8 copy.22
  1.4 0.7 fusion.17
  2.1 0.6 reduce-window.6
  2.7 0.2 slice_reduce_fusion
  2.9 0.8 fusion.16
  3.7 0.7 compare_select_fusion
  4.4 0.0 copy-start.1
  4.4 1.6 %copy-done.1 = f32[64,64,128]{2,1,0:T(8,128)S(1)} copy-done((f32[64,64,128]{2,1,0:T(8,128)S(1)}, f32[64,64,128]{2,1,0:T(8,128)}, u32[]{:S(2)}) %copy-start.1) | copy-done | bytes 2097176
  6.0 2.2 %shard_map.129.refs_1_ = f32[64,128]{1,0:T(8,128)S(1)} custom-call(f32[64,64,128]{2,1,0:T(8,128)S(1)} %copy-done.1), custom_call_target="tpu_custom_call" | custom-call | tf_op jit(solution)/shard_map/pallas_call | solution.py:231
  8.2 0.0 copy-start.2
  8.2 9.3 %shard_map.130 = (f32[64,128]{1,0:T(8,128)S(1)}, f32[64,128]{1,0:T(8,128)S(1)}, f32[64,128]{1,0:T(8,128)S(1)}, f32[64,128]{1,0:T(8,128)S(1)}) custom-call(f32[64,64,128]{2,1,0:T(8,128)S(1)} %copy-done.1, f32[64,128]{1,0:T(8,128)S(1)} %shard_map.129.refs_1_), custom_call_target="tpu_custom_call" | custom-call | tf_op jit(solution)/shard_map/pallas_call | solution.py:352
  17.5 0.1 copy.30.wo_ref
  17.7 0.1 copy.25
  17.8 1.2 scatter_custom_fusion
  19.0 0.1 reshape.94
  19.2 0.1 copy.23
  19.3 9.4 %shard_map.131 = (f32[64,64,128]{2,1,0:T(8,128)S(1)}, f32[64,128]{1,0:T(8,128)S(1)}) custom-call(f32[64,64,128]{2,1,0:T(8,128)S(1)} %copy-done.2, f32[64,128]{1,0:T(8,128)S(1)} %get-tuple-element.30.n_ref, f32[64,128]{1,0:T(8,128)S(1)} %get-tuple-element.31.s_ref, f32[64,128]{1,0:T(8,128)S(1)} %get-tuple-element.32.l_ref, ...), custom_call_target="tpu_custom_call" | custom-call | tf_op jit(solution)/shard_map/pallas_call | solution.py:231
  28.7 9.0 %shard_map.132 = (f32[64,128]{1,0:T(8,128)S(1)}, f32[64,128]{1,0:T(8,128)S(1)}, f32[64,128]{1,0:T(8,128)S(1)}, f32[64,128]{1,0:T(8,128)S(1)}, s32[32,1,64]{2,1,0:T(1,128)S(1)}) custom-call(f32[64,64,128]{2,1,0:T(8,128)S(1)} %get-tuple-element.34.refs_0_.x_ref.v_ref, f32[64,128]{1,0:T(8,128)S(1)} %get-tuple-element.35.refs_1_, s32[32,1,64]{2,1,0:T(1,128)S(1)} %bitcast.49), custom_call_target="tpu_custom_call" | custom-call | tf_op jit(solution)/shard_map/pallas_call | solution.py:352
  37.7 0.0 copy-start.3
  37.7 1.3 copy-done.3
  39.0 0.5 broadcast.119
  39.5 0.7 reduce.5
  40.2 0.2 reshape.95
  40.4 0.0 copy-start.10
  40.4 0.0 copy-start.11
  40.4 0.0 copy-start.12
  40.4 0.1 copy.27
  40.5 1.6 %copy-done.4 = f32[64,64,128]{2,1,0:T(8,128)S(1)} copy-done((f32[64,64,128]{2,1,0:T(8,128)S(1)}, f32[64,64,128]{2,1,0:T(8,128)}, u32[]{:S(2)}) %copy-start.4) | copy-done | bytes 2097176
  42.1 12.4 %shard_map.133.refs_0_ = f32[32,8,128]{2,1,0:T(8,128)S(1)} custom-call(f32[64,64,128]{2,1,0:T(8,128)S(1)} %copy-done.4, f32[64,128]{1,0:T(8,128)S(1)} %get-tuple-element.36.n_ref, f32[64,128]{1,0:T(8,128)S(1)} %get-tuple-element.37.s_ref, f32[64,128]{1,0:T(8,128)S(1)} %get-tuple-element.38.l_ref, f32[64,128]{1,0:T(8,128)S(1)} %get-tuple-element.39.r_ref, ...), custom_call_target="tpu_custom_call" | custom-call | tf_op jit(solution)/shard_map/pallas_call | solution.py:231
  54.5 9.4 %shard_map.134 = f32[32,8,128]{2,1,0:T(8,128)S(1)} custom-call(f32[32,8,128]{2,1,0:T(8,128)S(1)} %shard_map.133.refs_0_), custom_call_target="tpu_custom_call" | custom-call | tf_op jit(solution)/shard_map/pallas_call | solution.py:352
  63.9 0.7 gather_fusion
  64.7 0.3 fusion.1
  65.0 0.0 copy-start.13
  65.0 0.3 broadcast_select_fusion.1
  65.3 1.6 %scatter_custom_fusion.1 = f32[256,128]{1,0:T(8,128)S(1)} fusion(s32[256]{0:T(256)S(1)} %bitcast.54, f32[256,64]{1,0:T(8,128)S(1)} %get-tuple-element.59, f32[]{:T(128)} %constant.40, f32[256,64]{1,0:T(8,128)S(1)} %get-tuple-element.58, f32[]{:T(128)} %constant.12.clone.1), kind=kCustom, calls=%fused_computation.8 | custom fusion | flops 65536 | bytes 393224 | tf_op jit(solution)/shard_map/scatter-add | solution.py:453
  66.9 0.0 copy-start.5
  66.9 9.4 %shard_map.135.pulled_ref = f32[32,8,128]{2,1,0:T(8,128)S(1)} custom-call(f32[32,8,128]{2,1,0:T(8,128)S(1)} %bitcast.46), custom_call_target="tpu_custom_call" | custom-call | tf_op jit(solution)/shard_map/pallas_call | solution.py:352
  76.3 8.4 %shard_map.136 = (f32[64,64,128]{2,1,0:T(8,128)S(1)}, f32[64,128]{1,0:T(8,128)S(1)}) custom-call(f32[32,8,128]{2,1,0:T(8,128)S(1)} %shard_map.135.pulled_ref, s32[4,512]{1,0:T(4,128)S(1)} %bitcast.48), custom_call_target="tpu_custom_call" | custom-call | tf_op jit(solution)/shard_map/pallas_call | solution.py:231
  84.7 6.7 %shard_map.137 = (f32[64,128]{1,0:T(8,128)S(1)}, f32[64,128]{1,0:T(8,128)S(1)}, f32[64,128]{1,0:T(8,128)S(1)}, f32[64,128]{1,0:T(8,128)S(1)}) custom-call(f32[64,64,128]{2,1,0:T(8,128)S(1)} %get-tuple-element.41.refs_0_.x_ref, f32[64,128]{1,0:T(8,128)S(1)} %get-tuple-element.42.refs_1_), custom_call_target="tpu_custom_call" | custom-call | tf_op jit(solution)/shard_map/pallas_call | solution.py:352
  91.5 14.1 %shard_map.138 = (f32[64,64,128]{2,1,0:T(8,128)S(1)}, f32[64,128]{1,0:T(8,128)S(1)}, f32[512,128]{1,0:T(8,128)S(1)}) custom-call(f32[64,64,128]{2,1,0:T(8,128)S(1)} %copy-done.5, f32[64,64,128]{2,1,0:T(8,128)} %copy-done.6, f32[64,128]{1,0:T(8,128)S(1)} %get-tuple-element.43.n_ref, f32[64,128]{1,0:T(8,128)S(1)} %get-tuple-element.44.s_ref, ...), custom_call_target="tpu_custom_call" | custom-call | tf_op jit(solution)/shard_map/pallas_call | solution.py:231
  105.7 6.7 %shard_map.139 = (f32[64,128]{1,0:T(8,128)S(1)}, f32[64,128]{1,0:T(8,128)S(1)}, f32[64,128]{1,0:T(8,128)S(1)}, f32[64,128]{1,0:T(8,128)S(1)}) custom-call(f32[64,64,128]{2,1,0:T(8,128)S(1)} %get-tuple-element.47.refs_0_.x_ref, f32[64,128]{1,0:T(8,128)S(1)} %get-tuple-element.48.refs_1_), custom_call_target="tpu_custom_call" | custom-call | tf_op jit(solution)/shard_map/pallas_call | solution.py:352
  112.4 13.6 %shard_map.140 = (f32[64,64,128]{2,1,0:T(8,128)}, f32[64,128]{1,0:T(8,128)}, f32[512,128]{1,0:T(8,128)S(1)}) custom-call(f32[64,64,128]{2,1,0:T(8,128)S(1)} %copy-done.2, f32[64,64,128]{2,1,0:T(8,128)S(1)} %get-tuple-element.47.refs_0_.x_ref, f32[64,128]{1,0:T(8,128)S(1)} %get-tuple-element.49.n_ref, f32[64,128]{1,0:T(8,128)S(1)} %get-tuple-element.50.s_ref, ...), custom_call_target="tpu_custom_call" | custom-call | tf_op jit(solution)/shard_map/pallas_call | solution.py:231
  126.0 12.0 %shard_map.141 = f32[32,16,128]{2,1,0:T(8,128)S(1)} custom-call(f32[32,16,128]{2,1,0:T(8,128)S(1)} %bitcast.39), custom_call_target="tpu_custom_call" | custom-call | tf_op jit(solution)/shard_map/pallas_call | solution.py:352
  138.1 12.0 %shard_map.142 = f32[32,16,128]{2,1,0:T(8,128)S(1)} custom-call(f32[16,128]{1,0:T(8,128)S(1)} %broadcast_multiply_fusion.refs_0_), custom_call_target="tpu_custom_call" | custom-call | tf_op jit(solution)/shard_map/pallas_call | solution.py:352
  150.1 0.1 fusion.20
  150.3 0.8 copy.36
  151.1 0.8 copy.35
  (24 shorter events, 0.2 us)
Async XLA Ops:
  0.6 64.0 %copy-start = (f32[128,64]{0,1:T(8,128)S(1)}, f32[128,64]{0,1:T(8,128)}, u32[]{:S(2)}) copy-start(f32[128,64]{0,1:T(8,128)} %param.14) | copy-start | bytes 98308
  4.4 1.6 %copy-start.1 = (f32[64,64,128]{2,1,0:T(8,128)S(1)}, f32[64,64,128]{2,1,0:T(8,128)}, u32[]{:S(2)}) copy-start(f32[64,64,128]{2,1,0:T(8,128)} %v_ref.1) | copy-start | bytes 6291460
  6.0 11.5 %copy-start.8 = (bf16[512,64]{0,1:T(8,128)(2,1)S(1)}, bf16[512,64]{0,1:T(8,128)(2,1)}, u32[]{:S(2)}) copy-start(bf16[512,64]{0,1:T(8,128)(2,1)} %param.13) | copy-start | bytes 196612
  6.0 11.6 %copy-start.9 = (s32[256,4]{0,1:T(4,128)S(1)}, s32[256,4]{0,1:T(4,128)}, u32[]{:S(2)}) copy-start(s32[256,4]{0,1:T(4,128)} %param.18) | copy-start | bytes 12292
  6.0 13.2 %copy-start.7 = (bf16[64,512]{1,0:T(8,128)(2,1)S(1)}, bf16[64,512]{1,0:T(8,128)(2,1)}, u32[]{:S(2)}) copy-start(bf16[64,512]{1,0:T(8,128)(2,1)} %wi_ref.3) | copy-start | bytes 196612
  8.2 11.1 %copy-start.2 = (f32[64,64,128]{2,1,0:T(8,128)S(1)}, f32[64,64,128]{2,1,0:T(8,128)}, u32[]{:S(2)}) copy-start(f32[64,64,128]{2,1,0:T(8,128)} %v_ref.1) | copy-start | bytes 6291460
  37.7 1.3 copy-start.3
  40.4 24.2 %copy-start.10 = (f32[256,128]{1,0:T(8,128)S(1)}, f32[256,128]{1,0:T(8,128)}, u32[]{:S(2)}) copy-start(f32[256,128]{1,0:T(8,128)} %param.16) | copy-start | bytes 393220
  40.4 24.2 %copy-start.11 = (s32[256]{0:T(256)S(1)}, s32[256]{0:T(256)}, u32[]{:S(2)}) copy-start(s32[256]{0:T(256)} %param.19) | copy-start | bytes 3076
  40.4 24.2 %copy-start.12 = (f32[128]{0:T(128)S(1)}, f32[128]{0:T(128)}, u32[]{:S(2)}) copy-start(f32[128]{0:T(128)} %param.15) | copy-start | bytes 1540
  40.5 1.6 %copy-start.4 = (f32[64,64,128]{2,1,0:T(8,128)S(1)}, f32[64,64,128]{2,1,0:T(8,128)}, u32[]{:S(2)}) copy-start(f32[64,64,128]{2,1,0:T(8,128)} %copy-done.3) | copy-start | bytes 6291460
  65.0 40.6 %copy-start.13 = (f32[256,128]{1,0:T(8,128)}, f32[256,128]{1,0:T(8,128)S(1)}, u32[]{:S(2)}) copy-start(f32[256,128]{1,0:T(8,128)S(1)} %fusion.1) | copy-start | bytes 393220
  66.9 24.7 %copy-start.5 = (f32[64,64,128]{2,1,0:T(8,128)S(1)}, f32[64,64,128]{2,1,0:T(8,128)}, u32[]{:S(2)}) copy-start(f32[64,64,128]{2,1,0:T(8,128)} %copy-done.3) | copy-start | bytes 6291460
  84.7 6.8 %copy-start.6 = (f32[64,64,128]{2,1,0:T(8,128)}, f32[64,64,128]{2,1,0:T(8,128)S(1)}, u32[]{:S(2)}) copy-start(f32[64,64,128]{2,1,0:T(8,128)S(1)} %get-tuple-element.41.refs_0_.x_ref) | copy-start | bytes 6291460
